TPU v7x, 512 devices: a whole 4x8x8 slice. The times are simulated.
512 devices in a mesh: ulysses: 8 (over x, y_lo), blk: 8 (over z), tensor: 8 (over y_hi, core).
Axes of the slice: x: 4, y: 8 (y_hi: 4, y_lo: 2; y = y_hi * 2 + y_lo), z: 8, core: 2. Of those that a mesh axis runs over, the one named last changes fastest.
Arguments:
- tokens: bfloat16 [4096, 3072], P(('ulysses', 'blk'), 'tensor'), may hold values from -12 to 12
- cond: bfloat16 [3072], replicated, may hold values from -4 to 4
- mod_weight: bfloat16 [3072, 18432], P(None, ('ulysses', 'blk', 'tensor')), may hold values from -0.109375 to 0.109375
- qkv_weight: bfloat16 [3072, 3, 3072], P('tensor', None, 'ulysses'), as said below
- q_gain: float32 [128], replicated, may hold values from 1.2 to 3.4, as said below
- k_gain: float32 [128], replicated, may hold values from 1.2 to 3.4, as said below
- out_weight: bfloat16 [3072, 3072], P('ulysses', 'tensor'), may hold values from -0.109375 to 0.109375
- up_weight: bfloat16 [3072, 12288], P('tensor', 'ulysses'), may hold values from -0.109375 to 0.109375
- down_weight: bfloat16 [12288, 3072], P('ulysses', 'tensor'), may hold values from -0.0546875 to 0.0546875
Outputs:
- block_out: float32 [4096, 3072], P(('ulysses', 'blk'), 'tensor')
Inputs may be any that keep to these rules, and one draw needn't show every extreme that they name: `qkv_weight`: entries lie within four times 3072 ** -0.5 of zero. `q_gain`: positive gains. `k_gain`: positive gains.
All inputs are finite; a program needn't handle non-finite values.
Results may differ from a plain program's by a relative error of at most 0.011.
Values may be sent and summed in bfloat16 or wider, within the bound.
A program may use at most 64 MiB of HBM per device.

v0:
```python
import math

import jax
import jax.numpy as jnp
from jax import lax
from jax.sharding import PartitionSpec as P


def moments_norm(values, shift_row, scale_row, features):
    sums = lax.psum((jnp.sum(values, axis=-1), jnp.sum(values * values, axis=-1)), "tensor")
    average = sums[0][:, None] / features
    variance = sums[1][:, None] / features - average * average
    normal_rows = (values - average) * lax.rsqrt(variance + 1e-06)
    return (normal_rows * (1.0 + scale_row) + shift_row).astype(jnp.bfloat16)


def spread_rows(values):
    return lax.all_gather(values, "ulysses", axis=0, tiled=True)


def head_norm(values, gains):
    return values * lax.rsqrt(jnp.mean(values * values, axis=-1, keepdims=True) + 1e-06) * gains


def make_absorb(queries, score_scale, running, kv_block):
    keys_part, values_part = kv_block
    top_score, total_weight, summed = running
    scores = (
        jnp.einsum("qhd,khd->qhk", queries, keys_part, preferred_element_type=jnp.float32)
        * score_scale
    )
    new_top = jnp.max(scores, axis=-1)
    decay = jnp.exp(top_score - new_top)
    weights = jnp.exp(scores - new_top[..., None])
    total_weight = total_weight * decay + jnp.sum(weights, axis=-1)
    summed = summed * decay[..., None] + jnp.einsum(
        "qhk,khd->qhd",
        weights.astype(jnp.bfloat16),
        values_part,
        preferred_element_type=jnp.float32,
    )
    return (new_top, total_weight, summed)


def empty_state(row_count, heads_local, head_size):
    return (
        jnp.full((row_count, heads_local), -jnp.inf, jnp.float32),
        jnp.zeros((row_count, heads_local), jnp.float32),
        jnp.zeros((row_count, heads_local, head_size), jnp.float32),
    )


def on_device(
    tokens, cond, mod_weight, qkv_weight, q_gain, k_gain, out_weight, up_weight, down_weight
):
    tensor_size = lax.axis_size("tensor")
    tensor_pos = lax.axis_index("tensor")
    width = tokens.shape[1]
    features = width * tensor_size
    activated = jax.nn.silu(cond.astype(jnp.float32)).astype(jnp.bfloat16)
    local_mod = jnp.dot(activated[None, :], mod_weight, preferred_element_type=jnp.float32)[0]
    full_mod = lax.all_gather(local_mod, ("ulysses", "blk", "tensor"), axis=0, tiled=True).reshape(
        6, features
    )
    own_mod = lax.dynamic_slice_in_dim(full_mod, tensor_pos * width, width, 1)
    resid = tokens.astype(jnp.float32)
    normed = moments_norm(resid, own_mod[0], own_mod[1], features)
    gathered = spread_rows(normed)
    group_rows = gathered.shape[0]
    attn_rows = group_rows // tensor_size
    inner_local = qkv_weight.shape[2]
    head_size = q_gain.shape[0]
    heads_local = inner_local // head_size
    flat_qkv = qkv_weight.reshape(width, 3 * inner_local)
    projected = (
        lax.psum_scatter(
            jnp.dot(gathered, flat_qkv, preferred_element_type=jnp.float32).astype(jnp.bfloat16),
            "tensor",
            scatter_dimension=0,
            tiled=True,
        )
        .astype(jnp.float32)
        .reshape(attn_rows, 3, heads_local, head_size)
    )
    queries = head_norm(projected[:, 0], q_gain).astype(jnp.bfloat16)
    keys_local = head_norm(projected[:, 1], k_gain).astype(jnp.bfloat16)
    values_local = projected[:, 2].astype(jnp.bfloat16)
    score_scale = 1.0 / math.sqrt(head_size)
    state = make_absorb(
        queries,
        score_scale,
        empty_state(attn_rows, heads_local, head_size),
        (
            lax.all_gather(keys_local, ("blk", "tensor"), axis=0, tiled=True),
            lax.all_gather(values_local, ("blk", "tensor"), axis=0, tiled=True),
        ),
    )
    local_context = (
        (state[2] / state[1][..., None]).astype(jnp.bfloat16).reshape(attn_rows, inner_local)
    )
    context = lax.all_gather(local_context, "tensor", axis=0, tiled=True)
    attended = lax.psum_scatter(
        jnp.dot(context, out_weight, preferred_element_type=jnp.float32).astype(jnp.bfloat16),
        "ulysses",
        scatter_dimension=0,
        tiled=True,
    ).astype(jnp.float32)
    mixed = resid + own_mod[2] * attended
    normed_two = moments_norm(mixed, own_mod[3], own_mod[4], features)
    gathered_two = spread_rows(normed_two)
    hidden = lax.psum_scatter(
        jnp.dot(gathered_two, up_weight, preferred_element_type=jnp.float32).astype(jnp.bfloat16),
        "tensor",
        scatter_dimension=0,
        tiled=True,
    ).astype(jnp.float32)
    activ = jax.nn.gelu(hidden, approximate=True).astype(jnp.bfloat16)
    activ_rows = lax.all_gather(activ, "tensor", axis=0, tiled=True)
    feedforward = lax.psum_scatter(
        jnp.dot(activ_rows, down_weight, preferred_element_type=jnp.float32).astype(jnp.bfloat16),
        "ulysses",
        scatter_dimension=0,
        tiled=True,
    ).astype(jnp.float32)
    return mixed + own_mod[5] * feedforward


def solution(mesh):
    return jax.shard_map(
        on_device,
        mesh=mesh,
        in_specs=(
            P(("ulysses", "blk"), "tensor"),
            P(),
            P(None, ("ulysses", "blk", "tensor")),
            P("tensor", None, "ulysses"),
            P(),
            P(),
            P("ulysses", "tensor"),
            P("tensor", "ulysses"),
            P("ulysses", "tensor"),
        ),
        out_specs=P(("ulysses", "blk"), "tensor"),
        check_vma=False,
    )
```

profile of v0, /device:TPU:1, one launch (start us, length us, event | category | flops | bytes accessed | tf_op | source)
XLA Modules:
  0.0 760.5 jit_solution(16687946360828850503)
XLA Ops:
  7.4 1.1 convolution_bitcast_fusion
  10.4 20.4 %all-reduce.3 = (f32[64]{0:T(128)S(1)}, f32[64]{0:T(128)S(1)}) all-reduce(f32[64]{0:T(128)S(1)} %get-tuple-element.16, f32[64]{0:T(128)S(1)} %get-tuple-element.15), channel_id=1, replica_groups=mesh['ulysses'=8,'blk'=8,'tensor'=8] {'tensor'}, use_global_device_ids=true, to_apply=%region_3.4 | all-reduce | flops 128 | bytes 1024 | tf_op jit(solution)/shard_map/psum | solution.py:10
  30.8 2.5 copy.12
  33.3 249.5 %all-reduce.6.cloned.1.call-done = f32[6,3072]{1,0:T(8,128)} async-done(((f32[6,3072]{1,0:T(8,128)}), f32[6,3072]{1,0:T(8,128)}) %all-reduce.6.cloned.1.call-update) | async-done | bytes 73744
  284.8 24.4 %all_gather.22 = bf16[512,384]{1,0:T(8,128)(2,1)S(1)} all-gather(bf16[64,384]{1,0:T(8,128)(2,1)S(1)} %fusion.41), channel_id=1, replica_groups=mesh['ulysses'=8,'blk'=8,'tensor'=8] {'ulysses'}, dimensions={0}, use_global_device_ids=true | all-gather | bytes 442368 | tf_op jit(solution)/shard_map/all_gather | solution.py:18
  309.2 1.8 convolution_convert_fusion.1
  311.1 39.6 %reduce-scatter.5.cloned.1.call-done = bf16[64,1152]{1,0:T(8,128)(2,1)} async-done(((bf16[512,1152]{1,0:T(8,128)(2,1)}), bf16[64,1152]{1,0:T(8,128)(2,1)}) %reduce-scatter.5.cloned.1.call-update) | async-done | bytes 147472 | tf_op jit(solution)/shard_map/reduce_scatter | solution.py:76
  353.3 86.5 %all-gather.5.cloned.1.call-done = bf16[4096,3,128]{2,0,1:T(8,128)(2,1)} async-done(((bf16[64,3,128]{2,0,1:T(8,128)(2,1)}), bf16[4096,3,128]{2,0,1:T(8,128)(2,1)}) %all-gather.5.cloned.1.call-update) | async-done | bytes 3145744 | tf_op jit(solution)/shard_map/all_gather | solution.py:94
  439.8 3.2 fusion.54
  443.0 1.7 copy-done.1
  445.3 79.5 %all-gather.9.cloned.1.call-done = bf16[4096,1,3,128]{3,0,2,1:T(8,128)(2,1)} async-done(((bf16[64,1,3,128]{3,0,2,1:T(8,128)(2,1)}), bf16[4096,1,3,128]{3,0,2,1:T(8,128)(2,1)}) %all-gather.9.cloned.1.call-update) | async-done | bytes 3145744 | tf_op jit(solution)/shard_map/all_gather | solution.py:95
  524.8 3.7 fusion.27
  528.5 14.9 %all_gather.25 = bf16[512,384]{1,0:T(8,128)(2,1)S(1)} all-gather(bf16[64,384]{1,0:T(8,128)(2,1)S(1)} %bitcast.60), channel_id=1, replica_groups=mesh['ulysses'=8,'blk'=8,'tensor'=8] {'tensor'}, dimensions={0}, use_global_device_ids=true | all-gather | bytes 442368 | tf_op jit(solution)/shard_map/all_gather | solution.py:101
  543.4 1.1 convolution_convert_fusion.3
  544.6 34.7 %reduce-scatter.7.cloned.1.call-done = bf16[64,384]{1,0:T(8,128)(2,1)} async-done(((bf16[512,384]{1,0:T(8,128)(2,1)}), bf16[64,384]{1,0:T(8,128)(2,1)}) %reduce-scatter.7.cloned.1.call-update) | async-done | bytes 49168 | tf_op jit(solution)/shard_map/reduce_scatter | solution.py:102
  580.3 19.2 %all-reduce.2 = (f32[64]{0:T(128)S(1)}, f32[64]{0:T(128)S(1)}) all-reduce(f32[64]{0:T(128)S(1)} %get-tuple-element.8, f32[64]{0:T(128)S(1)} %get-tuple-element.7), channel_id=1, replica_groups=mesh['ulysses'=8,'blk'=8,'tensor'=8] {'tensor'}, use_global_device_ids=true, to_apply=%region_13.14 | all-reduce | flops 128 | bytes 1024 | tf_op jit(solution)/shard_map/psum | solution.py:10
  600.4 23.5 %all_gather.26 = bf16[512,384]{1,0:T(8,128)(2,1)S(1)} all-gather(bf16[64,384]{1,0:T(8,128)(2,1)S(1)} %add_convert_fusion), channel_id=1, replica_groups=mesh['ulysses'=8,'blk'=8,'tensor'=8] {'ulysses'}, dimensions={0}, use_global_device_ids=true | all-gather | bytes 442368 | tf_op jit(solution)/shard_map/all_gather | solution.py:18
  624.0 2.1 convolution_convert_fusion
  626.2 46.9 %reduce-scatter.9.cloned.1.call-done = bf16[64,1536]{1,0:T(8,128)(2,1)} async-done(((bf16[512,1536]{1,0:T(8,128)(2,1)}), bf16[64,1536]{1,0:T(8,128)(2,1)}) %reduce-scatter.9.cloned.1.call-update) | async-done | bytes 196624 | tf_op jit(solution)/shard_map/reduce_scatter | solution.py:111
  673.1 1.7 fusion.37
  674.9 36.5 %all-gather.7.cloned.1.call-done = bf16[512,1536]{1,0:T(8,128)(2,1)} async-done(((bf16[64,1536]{1,0:T(8,128)(2,1)}), bf16[512,1536]{1,0:T(8,128)(2,1)}) %all-gather.7.cloned.1.call-update) | async-done | bytes 1572880 | tf_op jit(solution)/shard_map/all_gather | solution.py:118
  711.4 3.1 convolution_convert_fusion.2
  714.6 37.6 %reduce-scatter.11.cloned.1.call-done = bf16[64,384]{1,0:T(8,128)(2,1)} async-done(((bf16[512,384]{1,0:T(8,128)(2,1)}), bf16[64,384]{1,0:T(8,128)(2,1)}) %reduce-scatter.11.cloned.1.call-update) | async-done | bytes 49168 | tf_op jit(solution)/shard_map/reduce_scatter | solution.py:119
  752.1 1.5 multiply_add_fusion
  (53 shorter events, 9.9 us)
Async XLA Ops:
  6.5 617.4 %copy-start = (bf16[384,1536]{1,0:T(8,128)(2,1)S(1)}, bf16[384,1536]{1,0:T(8,128)(2,1)}, u32[]{:S(2)}) copy-start(bf16[384,1536]{1,0:T(8,128)(2,1)} %param.16) | copy-start | bytes 3538948
  6.5 276.3 %all-reduce.6.cloned.1.call-start = ((), (), s32[]{:S(2)}) async-start(), calls=%async_computation.11 | async-start | bytes 196608
  9.4 341.2 %reduce-scatter.5.cloned.1.call-start = ((), (), s32[]{:S(2)}) async-start(), calls=%async_computation.4 | async-start | bytes 1327104 | tf_op jit(solution)/shard_map/reduce_scatter | solution.py:76
  33.3 318.5 %copy-start.5 = (f32[128]{0:T(128)S(1)}, f32[128]{0:T(128)}, u32[]{:S(2)}) copy-start(f32[128]{0:T(128)} %param.14) | copy-start | bytes 1540
  33.3 406.5 %copy-start.6 = (f32[128]{0:T(128)S(1)}, f32[128]{0:T(128)}, u32[]{:S(2)}) copy-start(f32[128]{0:T(128)} %param.13) | copy-start | bytes 1540
  311.0 128.8 %all-gather.5.cloned.1.call-start = ((), (), s32[]{:S(2)}) async-start(), calls=%async_computation.5 | async-start | bytes 3194880 | tf_op jit(solution)/shard_map/all_gather | solution.py:94
  352.5 172.3 %all-gather.9.cloned.1.call-start = ((), (), s32[]{:S(2)}) async-start(), calls=%async_computation.10 | async-start | bytes 3194880 | tf_op jit(solution)/shard_map/all_gather | solution.py:95
  353.2 226.1 %reduce-scatter.7.cloned.1.call-start = ((), (), s32[]{:S(2)}) async-start(), calls=%async_computation.6 | async-start | bytes 442368 | tf_op jit(solution)/shard_map/reduce_scatter | solution.py:102
  443.0 1.7 copy-start.1
  524.8 18.6 %copy-start.4 = (bf16[384,384]{1,0:T(8,128)(2,1)S(1)}, bf16[384,384]{1,0:T(8,128)(2,1)}, u32[]{:S(2)}) copy-start(bf16[384,384]{1,0:T(8,128)(2,1)} %param.15) | copy-start | bytes 884740
  524.8 54.6 %copy-start.2 = (bf16[64,384]{1,0:T(8,128)(2,1)S(1)}, bf16[64,384]{1,0:T(8,128)(2,1)}, u32[]{:S(2)}) copy-start(bf16[64,384]{1,0:T(8,128)(2,1)} %param.9) | copy-start | bytes 147460
  544.6 166.9 %copy-start.7 = (bf16[1536,384]{1,0:T(8,128)(2,1)S(1)}, bf16[1536,384]{1,0:T(8,128)(2,1)}, u32[]{:S(2)}) copy-start(bf16[1536,384]{1,0:T(8,128)(2,1)} %param.17) | copy-start | bytes 3538948
  544.6 128.5 %reduce-scatter.9.cloned.1.call-start = ((), (), s32[]{:S(2)}) async-start(), calls=%async_computation.7 | async-start | bytes 1769472 | tf_op jit(solution)/shard_map/reduce_scatter | solution.py:111
  626.1 85.3 %all-gather.7.cloned.1.call-start = ((), (), s32[]{:S(2)}) async-start(), calls=%async_computation.8 | async-start | bytes 1769472 | tf_op jit(solution)/shard_map/all_gather | solution.py:118
  674.9 77.3 %copy-start.3 = (bf16[64,384]{1,0:T(8,128)(2,1)S(1)}, bf16[64,384]{1,0:T(8,128)(2,1)}, u32[]{:S(2)}) copy-start(bf16[64,384]{1,0:T(8,128)(2,1)} %reduce-scatter.7.cloned.1.call-done) | copy-start | bytes 147460
  674.9 77.3 %reduce-scatter.11.cloned.1.call-start = ((), (), s32[]{:S(2)}) async-start(), calls=%async_computation.9 | async-start | bytes 442368 | tf_op jit(solution)/shard_map/reduce_scatter | solution.py:119
Sparse Core Ops, SparseCore 0:
  12.3 270.5 all-reduce.5
  311.1 39.4 reduce-scatter.4
  354.0 85.6 all-gather.4
  443.0 81.7 all-gather.8
  544.7 34.6 reduce-scatter.6
  626.2 46.8 reduce-scatter.8
  675.2 36.1 all-gather.6
  714.7 37.3 reduce-scatter.10
where the time goes:
time: 765 us; the launch traced here: 760 us
  waiting for transfers between devices  611 us (80%)
  blocking collectives  102 us (13%)
  matrix products  16.3 us (2%)
  between operations  13.6 us (2%)
  other arithmetic  10.1 us (1%)
    unnamed x9, waiting for transfers between devices  250 us
    all_gather x1, waiting for transfers between devices, on_device(): lax.all_gather(keys_local, ('blk', 'tensor'), axis=0, tiled=True)  86.5 us
    all_gather x1, waiting for transfers between devices, on_device(): lax.all_gather(values_local, ('blk', 'tensor'), axis=0, tiled=True)  79.5 us
    all_gather x2, blocking collectives, spread_rows(): return lax.all_gather(values, 'ulysses', axis=0, tiled=True)  47.9 us
    reduce_scatter x1, waiting for transfers between devices, on_device(): lax.psum_scatter(jnp.dot(gathered_two, up_weight, preferred_element_type=...  46.9 us
    psum x2, blocking collectives, moments_norm(): lax.psum((jnp.sum(values, axis=-1), jnp.sum(values * values, axis=-1)), '...  39.6 us
    reduce_scatter x1, waiting for transfers between devices, on_device(): lax.psum_scatter(jnp.dot(gathered, flat_qkv, preferred_element_type=jnp.f...  39.6 us
    reduce_scatter x1, waiting for transfers between devices, on_device(): lax.psum_scatter(jnp.dot(activ_rows, down_weight, preferred_element_type=...  37.6 us
  transfers between devices with their start and end apart: 8, of which 8 were waited for; matrix products, arithmetic and copies ran while one was open for 1% of the time, Pallas kernels for 0%

commit v1 on v0

v1 whole, which is shorter than its diff:
```python
import functools
import math

import jax
import jax.numpy as jnp
from jax import lax
from jax.experimental import pallas as pl
from jax.experimental.pallas import tpu as pltpu
from jax.sharding import PartitionSpec as P

MESH = pl.DeviceIdType.MESH
F32 = jnp.float32
BF16 = jnp.bfloat16


def block_kernel(
    U, B, T,
    tokens, cond, mod_w, qkv_w, q_gain, k_gain, out_w, up_w, down_w,
    out,
    tok_own, tok_rx, mw, wq, wo, wu, wd,
    m_tx, m_a, m_d, m_b, m_u, m_c, modv,
    st_tx, st_rx, rs_tx, rs_rx, q_rx, kv_rx, o_tx, o_rx, ctx_rx,
    at_tx, at_rx, mix, s2_tx, s2_rx, n2_tx, n2_rx, up_tx, up_rx, act_rx, ff_tx, ff_rx,
    loc_sem, w_send, w_recv,
    tok_send, tok_recv, ma_send, ma_recv, mb_send, mb_recv, mc_send, mc_recv,
    st_send, st_recv, rs_send, rs_recv, q_send, q_recv, kv_send, kv_recv, o_send, o_recv,
    cx_send, cx_recv, at_send, at_recv, s2_send, s2_recv, n2_send, n2_recv,
    up_send, up_recv, ac_send, ac_recv, ff_send, ff_recv,
):
    C = 2
    H = T // C
    R, W = tokens.shape
    G = H * R
    features = W * T
    u = lax.axis_index("ulysses")
    b = lax.axis_index("blk")
    t = lax.axis_index("tensor")
    h = t // C
    c = lax.rem(t, C)
    mate = {"tensor": h * C + (1 - c)}
    uc = u // H
    ui = lax.rem(u, H)
    pending = []
    y_far = sorted(range(1, H), key=lambda k: -min(k, H - k))
    y_near = y_far[::-1]

    def rdma(src, dst, send, recv, dev):
        copy = pltpu.make_async_remote_copy(
            src_ref=src, dst_ref=dst, send_sem=send, recv_sem=recv,
            device_id=dev, device_id_type=MESH,
        )
        copy.start()
        pending.append((None, copy))

    def rdma_or_local(own, src, dst, send, recv, dev):
        copy = pltpu.make_async_remote_copy(
            src_ref=src, dst_ref=dst, send_sem=send, recv_sem=recv,
            device_id=dev, device_id_type=MESH,
        )

        @pl.when(own)
        def _():
            pltpu.make_async_copy(src, dst, recv).start()

        @pl.when(jnp.logical_not(own))
        def _():
            copy.start()

        pending.append((own, copy))

    def arrived(dst, recv):
        pltpu.make_async_copy(dst, dst, recv).wait()

    def y_peer(k):
        hp = lax.rem(h + k, H)
        return hp, {"tensor": hp * C + c}

    barrier = pltpu.get_barrier_semaphore()
    count = 0
    for k in range(1, B):
        pl.semaphore_signal(barrier, inc=1, device_id={"blk": lax.rem(b + k, B)}, device_id_type=MESH)
        count += 1
    for k in range(1, T):
        pl.semaphore_signal(barrier, inc=1, device_id={"tensor": lax.rem(t + k, T)}, device_id_type=MESH)
        count += 1
    for k in range(1, U):
        for cc in range(C):
            pl.semaphore_signal(
                barrier, inc=1,
                device_id={"ulysses": lax.rem(u + k, U), "tensor": h * C + cc},
                device_id_type=MESH,
            )
            count += 1

    local = [
        pltpu.make_async_copy(mod_w, mw, loc_sem.at[0]),
        pltpu.make_async_copy(tokens, tok_own, loc_sem.at[1]),
        pltpu.make_async_copy(qkv_w, wq.at[:, c], loc_sem.at[2]),
        pltpu.make_async_copy(out_w, wo.at[c], loc_sem.at[3]),
        pltpu.make_async_copy(up_w, wu.at[c], loc_sem.at[4]),
        pltpu.make_async_copy(down_w, wd.at[c], loc_sem.at[5]),
    ]
    for copy in local:
        copy.start()

    condf = cond[...].astype(F32)
    active = (condf * jax.nn.sigmoid(condf)).astype(BF16)
    local[0].wait()
    share = lax.dot_general(
        jnp.broadcast_to(active, (16, features)), mw[...],
        (((1,), (1,)), ((), ())), preferred_element_type=F32,
    )
    n_share = mod_w.shape[0]
    start = n_share * (b * T + t)
    lanes2 = lax.broadcasted_iota(jnp.int32, (n_share, 256), 1)
    rows2 = lax.broadcasted_iota(jnp.int32, (n_share, 256), 0)
    place = (lanes2 == rows2 + lax.rem(start, 128)).astype(F32)
    placed = jnp.dot(share[0:8], place, preferred_element_type=F32, precision=lax.Precision.HIGHEST)
    sub8 = lax.broadcasted_iota(jnp.int32, (8, 128), 0)
    tile = jnp.where(sub8 == 0, placed[:, 0:128], jnp.where(sub8 == 1, placed[:, 128:256], 0.0))
    m_tx[...] = tile
    m_a[b] = tile

    pl.semaphore_wait(barrier, count)

    for k in range(1, B):
        rdma(m_tx, m_a.at[b], ma_send.at[k], ma_recv.at[b], {"blk": lax.rem(b + k, B)})
    for up_ in range(U):
        rdma_or_local(
            jnp.logical_and(u == up_, c == uc),
            tokens, tok_rx.at[c, pl.ds(ui * R, R), :], tok_send.at[up_], tok_recv.at[c, ui],
            {"ulysses": up_, "tensor": h * C + uc},
        )
    rdma(qkv_w, wq.at[:, c], w_send.at[0], w_recv.at[0], mate)
    rdma(out_w, wo.at[c], w_send.at[1], w_recv.at[1], mate)
    rdma(up_w, wu.at[c], w_send.at[2], w_recv.at[2], mate)
    rdma(down_w, wd.at[c], w_send.at[3], w_recv.at[3], mate)

    per_u = n_share * B * T // 128
    m_d[...] = jnp.zeros_like(m_d)
    for k in range(B):
        if k:
            bp = lax.rem(b + k, B)
            arrived(m_a.at[bp], ma_recv.at[bp])
    for bp in range(B):
        row = (n_share * (bp * T + t)) // 128
        m_d[pl.ds(row, 1), :] += m_a[bp, 0:1, :]
        m_d[pl.ds(row + 1, 1), :] += m_a[bp, 1:2, :]
    m_b[t] = m_d[...]
    for k in range(1, T):
        rdma(m_d, m_b.at[t], mb_send.at[k], mb_recv.at[t], {"tensor": lax.rem(t + k, T)})

    for cc in range(C):
        for i in range(H):
            arrived(tok_rx.at[cc, pl.ds(i * R, R), :], tok_recv.at[cc, i])
    x0 = tok_rx[0].astype(F32)
    x1 = tok_rx[1].astype(F32)
    local_mean = (jnp.sum(x0, -1, keepdims=True) + jnp.sum(x1, -1, keepdims=True)) * (1.0 / (C * W))
    d0 = x0 - local_mean
    d1 = x1 - local_mean
    local_m2 = jnp.sum(d0 * d0, -1, keepdims=True) + jnp.sum(d1 * d1, -1, keepdims=True)
    lane = lax.broadcasted_iota(jnp.int32, (G, 128), 1)
    stats = jnp.where(lane == 0, local_mean, jnp.where(lane == 1, local_m2, 0.0))
    stats_t = jnp.transpose(stats)[0:8]
    st_tx[...] = stats_t
    st_rx[h] = stats_t
    for k in range(1, H):
        hp, dev = y_peer(k)
        rdma(st_tx, st_rx.at[h], st_send.at[k], st_recv.at[h], dev)

    for k in range(1, T):
        tp = lax.rem(t + k, T)
        arrived(m_b.at[tp], mb_recv.at[tp])
    dense = m_b[0]
    for tp in range(1, T):
        dense = dense + m_b[tp]
    m_u[...] = dense
    m_c[u] = dense
    for k in range(1, U):
        rdma(m_u, m_c.at[u], mc_send.at[k], mc_recv.at[u], {"ulysses": lax.rem(u + k, U)})

    for k in range(1, H):
        hp, _ = y_peer(k)
        arrived(st_rx.at[hp], st_recv.at[hp])
    mean = st_rx[0, 0:1, :]
    for hp in range(1, H):
        mean = mean + st_rx[hp, 0:1, :]
    mean = mean * (1.0 / H)
    m2 = jnp.zeros_like(mean)
    for hp in range(H):
        diff = st_rx[hp, 0:1, :] - mean
        m2 = m2 + st_rx[hp, 1:2, :] + (C * W) * diff * diff
    rstd = lax.rsqrt(m2 * (1.0 / features) + 1e-06)
    subg = lax.broadcasted_iota(jnp.int32, (128, G), 0)
    cols = jnp.transpose(jnp.where(subg == 0, mean, jnp.where(subg == 1, rstd, 0.0)))
    mean_c, rstd_c = cols[:, 0:1], cols[:, 1:2]

    for k in range(1, U):
        upk = lax.rem(u + k, U)
        arrived(m_c.at[upk], mc_recv.at[upk])
    for v in range(6):
        for k in range(C * W // 128):
            row = v * (features // 128) + h * (C * W // 128) + k
            modv[v:v + 1, 128 * k:128 * (k + 1)] = m_c[row // per_u, pl.ds(lax.rem(row, per_u), 1), :]

    n0 = ((x0 - mean_c) * rstd_c * (1.0 + modv[1:2, 0:W]) + modv[0:1, 0:W]).astype(BF16)
    n1 = ((x1 - mean_c) * rstd_c * (1.0 + modv[1:2, W:2 * W]) + modv[0:1, W:2 * W]).astype(BF16)

    local[2].wait()
    arrived(wq.at[:, 1 - c], w_recv.at[0])
    for g in range(3):
        part = jnp.dot(n0, wq[g, 0], preferred_element_type=F32)
        part = part + jnp.dot(n1, wq[g, 1], preferred_element_type=F32)
        rs_tx[g] = part.astype(BF16)
        for k in y_far:
            hp, dev = y_peer(k)
            rdma(rs_tx.at[g, pl.ds(hp * R, R), :], rs_rx.at[g, h], rs_send.at[g, k], rs_recv.at[g, h], dev)
        rs_rx[g, h] = rs_tx[g, pl.ds(h * R, R), :]

    slot = c * H + h
    heads = W // 128
    for g in range(3):
        for k in y_near:
            hp, _ = y_peer(k)
            arrived(rs_rx.at[g, hp], rs_recv.at[g, hp])
        total = rs_rx[g, 0].astype(F32)
        for hp in range(1, H):
            total = total + rs_rx[g, hp].astype(F32)
        if g < 2:
            gain = (q_gain if g == 0 else k_gain)[...]
            pieces = []
            for hd in range(heads):
                piece = total[:, 128 * hd:128 * (hd + 1)]
                ms = jnp.mean(piece * piece, axis=-1, keepdims=True)
                pieces.append(piece * lax.rsqrt(ms + 1e-06) * gain)
            total = jnp.concatenate(pieces, axis=1)
        if g == 0:
            q_rx[pl.ds(b * R, R), :] = total.astype(BF16)
            for k in range(1, B):
                rows = q_rx.at[pl.ds(b * R, R), :]
                rdma(rows, rows, q_send.at[k], q_recv.at[b], {"blk": lax.rem(b + k, B)})
        else:
            rows = kv_rx.at[g - 1, pl.ds(slot * R, R), :]
            kv_rx[g - 1, pl.ds(slot * R, R), :] = total.astype(BF16)
            for k in y_far:
                _, dev = y_peer(k)
                rdma(rows, rows, kv_send.at[g - 1, k], kv_recv.at[g - 1, slot], dev)
            rdma(rows, rows, kv_send.at[g - 1, 0], kv_recv.at[g - 1, slot], mate)
    for g in range(2):
        for k in y_near:
            hp, _ = y_peer(k)
            sp = c * H + hp
            rows = kv_rx.at[g, pl.ds(sp * R, R), :]
            arrived(rows, kv_recv.at[g, sp])
            rdma(rows, rows, kv_send.at[g, 4 + k], kv_recv.at[g, sp], mate)
    for k in range(1, B):
        bp = lax.rem(b + k, B)
        arrived(q_rx.at[pl.ds(bp * R, R), :], q_recv.at[bp])
    for g in range(2):
        for hp in range(H):
            sp = (1 - c) * H + hp
            arrived(kv_rx.at[g, pl.ds(sp * R, R), :], kv_recv.at[g, sp])

    scale = 1.0 / math.sqrt(128)
    QB = 128 if B * R % 128 == 0 else R

    def attend(qb, carry):
        at = pl.multiple_of(qb * QB, QB)
        lane_q = lax.broadcasted_iota(jnp.int32, (QB, 128), 1)
        tail = jnp.zeros((QB, 128), F32)
        for hd in range(heads):
            cut = slice(128 * hd, 128 * (hd + 1))
            s = lax.dot_general(
                q_rx[pl.ds(at, QB), cut], kv_rx[0, :, cut],
                (((1,), (1,)), ((), ())), preferred_element_type=F32,
            )
            top = jnp.max(s, axis=-1, keepdims=True).astype(BF16).astype(F32)
            p = jnp.exp((s - top) * scale)
            weight = jnp.sum(p, axis=-1, keepdims=True)
            o = jnp.dot(p.astype(BF16), kv_rx[1, :, cut], preferred_element_type=F32)
            o_tx[pl.ds(at, QB), cut] = o.astype(BF16)
            high = weight.astype(BF16).astype(F32)
            tail = jnp.where(lane_q == hd, top, tail)
            tail = jnp.where(lane_q == heads + hd, high, tail)
            tail = jnp.where(lane_q == 2 * heads + hd, weight - high, tail)
        o_tx[pl.ds(at, QB), W:W + 128] = tail.astype(BF16)
        return carry

    lax.fori_loop(0, B * R // QB, attend, 0)
    o_rx[b] = o_tx[pl.ds(b * R, R), :]
    for k in sorted(range(1, B), key=lambda k: -min(k, B - k)):
        bp = lax.rem(b + k, B)
        rdma(o_tx.at[pl.ds(bp * R, R), :], o_rx.at[b], o_send.at[k], o_recv.at[b], {"blk": bp})
    for k in range(1, B):
        bp = lax.rem(b + k, B)
        arrived(o_rx.at[bp], o_recv.at[bp])
    pieces = []
    for hd in range(heads):
        cut = slice(128 * hd, 128 * (hd + 1))
        tops = [o_rx[bp, :, W + hd:W + hd + 1].astype(F32) for bp in range(B)]
        top = functools.reduce(jnp.maximum, tops)
        num = jnp.zeros((R, 128), F32)
        den = jnp.zeros((R, 1), F32)
        for bp in range(B):
            share_b = jnp.exp((tops[bp] - top) * scale)
            num = num + share_b * o_rx[bp, :, cut].astype(F32)
            den = den + share_b * (
                o_rx[bp, :, W + heads + hd:W + heads + hd + 1].astype(F32)
                + o_rx[bp, :, W + 2 * heads + hd:W + 2 * heads + hd + 1].astype(F32)
            )
        pieces.append(num / den)
    mine = ctx_rx.at[pl.ds(h * R, R), :]
    ctx_rx[pl.ds(h * R, R), :] = jnp.concatenate(pieces, axis=1).astype(BF16)
    for k in y_far:
        _, dev = y_peer(k)
        rdma(mine, mine, cx_send.at[k], cx_recv.at[h], dev)
    local[3].wait()
    arrived(wo.at[1 - c], w_recv.at[1])
    for k in y_near:
        hp, _ = y_peer(k)
        arrived(ctx_rx.at[pl.ds(hp * R, R), :], cx_recv.at[hp])

    def to_owners(tx, rx, send, recv, cc):
        for hp in range(H):
            up_ = c * H + hp
            rdma_or_local(
                jnp.logical_and(up_ == u, c == cc),
                tx.at[cc, pl.ds(hp * R, R), :], rx.at[u], send.at[cc, hp], recv.at[u],
                {"ulysses": up_, "tensor": h * C + cc},
            )

    for cc in range(C):
        at_tx[cc] = jnp.dot(ctx_rx[...], wo[cc], preferred_element_type=F32).astype(BF16)
        to_owners(at_tx, at_rx, at_send, at_recv, cc)
    for up_ in range(U):
        arrived(at_rx.at[up_], at_recv.at[up_])
    attended = at_rx[0].astype(F32)
    for up_ in range(1, U):
        attended = attended + at_rx[up_].astype(F32)
    local[1].wait()
    own_cols = pl.ds(pl.multiple_of(c * W, 128), W)
    mixed = tok_own[...].astype(F32) + modv[2:3, own_cols] * attended
    mix[...] = mixed

    mean_l = jnp.sum(mixed, -1, keepdims=True) * (1.0 / W)
    diff = mixed - mean_l
    m2_l = jnp.sum(diff * diff, -1, keepdims=True)
    lane_r = lax.broadcasted_iota(jnp.int32, (R, 128), 1)
    st2 = jnp.where(lane_r == 0, mean_l, jnp.where(lane_r == 1, m2_l, 0.0))
    st2_t = jnp.transpose(jnp.concatenate([st2, jnp.zeros((128 - R, 128), F32)], axis=0))[0:8]
    s2_tx[...] = st2_t
    s2_rx[t] = st2_t
    for k in range(1, T):
        rdma(s2_tx, s2_rx.at[t], s2_send.at[k], s2_recv.at[t], {"tensor": lax.rem(t + k, T)})
    for k in range(1, T):
        tp = lax.rem(t + k, T)
        arrived(s2_rx.at[tp], s2_recv.at[tp])
    total = s2_rx[0]
    for tp in range(1, T):
        total = total + s2_rx[tp]
    mean2 = total[0:1] * (1.0 / T)
    m2 = total[1:2]
    for tp in range(T):
        dev2 = s2_rx[tp, 0:1, :] - mean2
        m2 = m2 + W * dev2 * dev2
    rstd2 = lax.rsqrt(m2 * (1.0 / features) + 1e-06)
    sub2 = lax.broadcasted_iota(jnp.int32, (128, 128), 0)
    cols2 = jnp.transpose(jnp.where(sub2 == 0, mean2, jnp.where(sub2 == 1, rstd2, 0.0)))
    normed = (mixed - cols2[0:R, 0:1]) * cols2[0:R, 1:2]
    n2_tx[...] = (normed * (1.0 + modv[4:5, own_cols]) + modv[3:4, own_cols]).astype(BF16)
    for up_ in range(U):
        rdma_or_local(
            jnp.logical_and(u == up_, c == uc),
            n2_tx, n2_rx.at[c, pl.ds(ui * R, R), :], n2_send.at[up_], n2_recv.at[c, ui],
            {"ulysses": up_, "tensor": h * C + uc},
        )
    local[4].wait()
    arrived(wu.at[1 - c], w_recv.at[2])
    for cc in range(C):
        for i in range(H):
            arrived(n2_rx.at[cc, pl.ds(i * R, R), :], n2_recv.at[cc, i])

    J = up_w.shape[1] // W
    for j in range(J):
        cut = slice(W * j, W * (j + 1))
        part = jnp.dot(n2_rx[0], wu[0, :, cut], preferred_element_type=F32)
        part = part + jnp.dot(n2_rx[1], wu[1, :, cut], preferred_element_type=F32)
        up_tx[j] = part.astype(BF16)
        for k in y_far:
            hp, dev = y_peer(k)
            rdma(up_tx.at[j, pl.ds(hp * R, R), :], up_rx.at[j, h], up_send.at[j, k], up_recv.at[j, h], dev)
        up_rx[j, h] = up_tx[j, pl.ds(h * R, R), :]
    for j in range(J):
        for k in y_near:
            hp, _ = y_peer(k)
            arrived(up_rx.at[j, hp], up_recv.at[j, hp])
        hidden = up_rx[j, 0].astype(F32)
        for hp in range(1, H):
            hidden = hidden + up_rx[j, hp].astype(F32)
        mine = act_rx.at[j, pl.ds(h * R, R), :]
        act_rx[j, pl.ds(h * R, R), :] = jax.nn.gelu(hidden, approximate=True).astype(BF16)
        for k in y_far:
            _, dev = y_peer(k)
            rdma(mine, mine, ac_send.at[j, k], ac_recv.at[j, h], dev)
    local[5].wait()
    arrived(wd.at[1 - c], w_recv.at[3])
    accs = [None] * C
    for j in range(J):
        for k in y_near:
            hp, _ = y_peer(k)
            arrived(act_rx.at[j, pl.ds(hp * R, R), :], ac_recv.at[j, hp])
        for cc in range(C):
            part = jnp.dot(act_rx[j], wd[cc, W * j:W * (j + 1), :], preferred_element_type=F32)
            accs[cc] = part if j == 0 else accs[cc] + part
    for cc in range(C):
        ff_tx[cc] = accs[cc].astype(BF16)
        to_owners(ff_tx, ff_rx, ff_send, ff_recv, cc)
    for up_ in range(U):
        arrived(ff_rx.at[up_], ff_recv.at[up_])
    feed = ff_rx[0].astype(F32)
    for up_ in range(1, U):
        feed = feed + ff_rx[up_].astype(F32)
    out[...] = mix[...] + modv[5:6, own_cols] * feed

    for own, copy in pending:
        if own is None:
            copy.wait_send()
        else:
            pl.when(jnp.logical_not(own))(copy.wait_send)


def on_device(
    tokens, cond, mod_weight, qkv_weight, q_gain, k_gain, out_weight, up_weight, down_weight
):
    U = lax.axis_size("ulysses")
    B = lax.axis_size("blk")
    T = lax.axis_size("tensor")
    H = T // 2
    R, W = tokens.shape
    G = H * R
    FFL = up_weight.shape[1]
    J = FFL // W
    dma = pltpu.SemaphoreType.DMA
    vmem = pltpu.VMEM
    any_spec = pl.BlockSpec(memory_space=pl.ANY)
    vm_spec = pl.BlockSpec(memory_space=pltpu.VMEM)
    return pl.pallas_call(
        functools.partial(block_kernel, U, B, T),
        out_shape=jax.ShapeDtypeStruct((R, W), F32),
        in_specs=[any_spec, vm_spec, any_spec, any_spec, vm_spec, vm_spec, any_spec, any_spec, any_spec],
        out_specs=vm_spec,
        scratch_shapes=[
            vmem((R, W), BF16),
            vmem((2, G, W), BF16),
            vmem((mod_weight.shape[1], mod_weight.shape[0]), BF16),
            vmem((3, 2, W, W), BF16),
            vmem((2, W, W), BF16),
            vmem((2, W, FFL), BF16),
            vmem((2, FFL, W), BF16),
            vmem((8, 128), F32),
            vmem((B, 8, 128), F32),
            vmem((24, 128), F32),
            vmem((T, 24, 128), F32),
            vmem((24, 128), F32),
            vmem((U, 24, 128), F32),
            vmem((8, 2 * W), F32),
            vmem((8, G), F32),
            vmem((H, 8, G), F32),
            vmem((3, G, W), BF16),
            vmem((3, H, R, W), BF16),
            vmem((B * R, W), BF16),
            vmem((2, T * R, W), BF16),
            vmem((B * R, W + 128), BF16),
            vmem((B, R, W + 128), BF16),
            vmem((G, W), BF16),
            vmem((2, G, W), BF16),
            vmem((U, R, W), BF16),
            vmem((R, W), F32),
            vmem((8, 128), F32),
            vmem((T, 8, 128), F32),
            vmem((R, W), BF16),
            vmem((2, G, W), BF16),
            vmem((J, G, W), BF16),
            vmem((J, H, R, W), BF16),
            vmem((J, G, W), BF16),
            vmem((2, G, W), BF16),
            vmem((U, R, W), BF16),
            dma((6,)), dma((4,)), dma((4,)),
            dma((U,)), dma((2, H)), dma((B,)), dma((B,)), dma((T,)), dma((T,)), dma((U,)), dma((U,)),
            dma((H,)), dma((H,)), dma((3, H)), dma((3, H)), dma((B,)), dma((B,)), dma((2, 8)), dma((2, T)), dma((B,)), dma((B,)),
            dma((H,)), dma((H,)), dma((2, H)), dma((U,)), dma((T,)), dma((T,)), dma((U,)), dma((2, H)),
            dma((J, H)), dma((J, H)), dma((J, H)), dma((J, H)), dma((2, H)), dma((U,)),
        ],
        compiler_params=pltpu.CompilerParams(
            collective_id=0, has_side_effects=True, vmem_limit_bytes=48 * 1024 * 1024
        ),
        name="block_kernel",
    )(
        tokens,
        cond.reshape(1, -1),
        mod_weight.T,
        qkv_weight.transpose(1, 0, 2),
        q_gain.reshape(1, -1),
        k_gain.reshape(1, -1),
        out_weight,
        up_weight,
        down_weight,
    )


def solution(mesh):
    return jax.shard_map(
        on_device,
        mesh=mesh,
        in_specs=(
            P(("ulysses", "blk"), "tensor"),
            P(),
            P(None, ("ulysses", "blk", "tensor")),
            P("tensor", None, "ulysses"),
            P(),
            P(),
            P("ulysses", "tensor"),
            P("tensor", "ulysses"),
            P("ulysses", "tensor"),
        ),
        out_specs=P(("ulysses", "blk"), "tensor"),
        check_vma=False,
    )
```

time: 765 us -> 155 us (0.20)
  waiting for transfers between devices: 611 us -> 0 us
  Pallas kernels: 0 us -> 145 us
  blocking collectives: 102 us -> 0 us
  matrix products: 16.3 us -> 0 us
  between operations: 13.6 us -> 0.02 us
  other arithmetic: 10.1 us -> 0 us
    unnamed x9 -> x0, waiting for transfers between devices: 250 us -> none
    all_gather x3 -> x0, waiting for transfers between devices: 202 us -> none  [the longest x1 86.5 us: on_device(): lax.all_gather(keys_local, ('blk', 'tensor'), axis=0, tiled=True)]
    reduce_scatter x4 -> x0, waiting for transfers between devices: 159 us -> none  [the longest x1 46.9 us: on_device(): lax.psum_scatter(jnp.dot(gathered_two, up_weight, preferred_element_type=...]
    pallas_call x0 -> x1, Pallas kernels: none -> 145 us  [on_device(): pl.pallas_call(functools.partial(block_kernel, U, B, T), out_shape=jax.Sh...]
    all_gather x3 -> x0, blocking collectives: 62.8 us -> none  [the longest x2 47.9 us: spread_rows(): return lax.all_gather(values, 'ulysses', axis=0, tiled=True)]
    psum x2 -> x0, blocking collectives: 39.6 us -> none  [moments_norm(): lax.psum((jnp.sum(values, axis=-1), jnp.sum(values * values, axis=-1)), '...]
    dot_general x7 -> x0, matrix products: 16.3 us -> none  [the longest x1 3.68 us: make_absorb(): jnp.einsum('qhk,khd->qhd', weights.astype(jnp.bfloat16), values_part, pre...]
  transfers between devices with their start and end apart: 8 -> 0, of which waited for: 8 -> 0; matrix products, arithmetic and copies ran while one was open for 1% -> 0% of each run, Pallas kernels for 0% -> 0%
where the time goes in v1:
time: 155 us; the launch traced here: 154 us
  Pallas kernels  145 us (94%)
  local copies, waits for them, and re-layouts  9.06 us (6%)
    pallas_call x1, Pallas kernels, on_device(): pl.pallas_call(functools.partial(block_kernel, U, B, T), out_shape=jax.Sh...  145 us
    unnamed x17, local copies, waits for them, and re-layouts  8.36 us

profile of v1, /device:TPU:1, one launch (start us, length us, event | category | flops | bytes accessed | tf_op | source)
XLA Modules:
  0.0 154.1 jit_solution(9216577386499661202)
XLA Ops:
  0.0 0.7 reshape.9.cond
  0.7 0.0 copy-start
  0.7 1.3 copy-done
  2.0 0.0 copy-start.1
  2.0 1.3 copy-done.1
  3.2 0.0 copy-start.2
  3.2 1.2 copy-done.2
  4.4 0.0 copy-start.3
  4.4 1.0 copy-done.3
  5.4 0.0 copy-start.4
  5.4 0.9 copy-done.4
  6.3 0.0 copy-start.5
  6.3 0.8 copy-done.5
  7.1 0.0 copy-start.6
  7.1 0.7 copy-done.6
  7.8 0.0 copy-start.7
  7.8 0.7 copy-done.7
  8.4 145.1 %block_kernel.1 = f32[64,384]{1,0:T(8,128)S(1)} custom-call(bf16[64,384]{1,0:T(8,128)(2,1)S(1)} %copy-done.5, bf16[1,3072]{1,0:T(2,128)(2,1)S(1)} %reshape.9.cond, bf16[36,3072]{1,0:T(8,128)(2,1)S(1)} %bitcast.5, bf16[3,384,384]{2,1,0:T(8,128)(2,1)S(1)} %bitcast.4, f32[1,128]{1,0:T(1,128)S(1)} %bitcast.6, f32[1,128]{1,0:T(1,128)S(1)} %bitcast.7, ...), custom_call_target="tpu_custom_call" | custom-call | tf_op jit(solution)/shard_map/block_kernel/pallas_call | solution.py:447
  153.5 0.6 copy.11
Async XLA Ops:
  0.7 1.3 copy-start
  2.0 1.3 copy-start.1
  3.2 1.2 copy-start.2
  4.4 1.0 copy-start.3
  5.4 0.9 copy-start.4
  6.3 0.8 copy-start.5
  7.1 0.7 copy-start.6
  7.8 0.7 copy-start.7

commit v2 on v1

--- a/solution.py
+++ b/solution.py
@@ -17,13 +17,13 @@
     U, B, T,
     tokens, cond, mod_w, qkv_w, q_gain, k_gain, out_w, up_w, down_w,
     out,
-    tok_own, tok_rx, mw, wq, wo, wu, wd,
+    tok_own, cond_v, qg_v, kg_v, tok_rx, mw, wq, wo, wu, wd,
     m_tx, m_a, m_d, m_b, m_u, m_c, modv,
-    st_tx, st_rx, rs_tx, rs_rx, q_rx, kv_rx, o_tx, o_rx, ctx_rx,
-    at_tx, at_rx, mix, s2_tx, s2_rx, n2_tx, n2_rx, up_tx, up_rx, act_rx, ff_tx, ff_rx,
+    st_tx, st_rx, rs_tx, rs_rb, rs_rx, q_rx, kv_rx, o_tx, o_rx, os_tx, os_rx, cf, cf_t, ctx_rx,
+    at_tx, at_rx, mix, s2_tx, s2_rx, n2_tx, n2_rx, up_tx, up_rb, up_rx, act_rx, ff_tx, ff_rx,
     loc_sem, w_send, w_recv,
     tok_send, tok_recv, ma_send, ma_recv, mb_send, mb_recv, mc_send, mc_recv,
-    st_send, st_recv, rs_send, rs_recv, q_send, q_recv, kv_send, kv_recv, o_send, o_recv,
+    st_send, st_recv, rs_send, rs_recv, q_send, q_recv, kv_send, kv_recv, km_send, km_recv, o_send, o_recv, os_send, os_recv,
     cx_send, cx_recv, at_send, at_recv, s2_send, s2_recv, n2_send, n2_recv,
     up_send, up_recv, ac_send, ac_recv, ff_send, ff_recv,
 ):
@@ -41,8 +41,6 @@
     uc = u // H
     ui = lax.rem(u, H)
     pending = []
-    y_far = sorted(range(1, H), key=lambda k: -min(k, H - k))
-    y_near = y_far[::-1]
 
     def rdma(src, dst, send, recv, dev):
         copy = pltpu.make_async_remote_copy(
@@ -74,6 +72,48 @@
     def y_peer(k):
         hp = lax.rem(h + k, H)
         return hp, {"tensor": hp * C + c}
+
+    hr, right = y_peer(1)
+    ho, _ = y_peer(2)
+    hl, left = y_peer(3)
+    R2 = R // 2
+
+    def gather_start(rows, send, recv):
+        mine = rows(h, 0, R)
+        rdma(mine, mine, send(0), recv(0), right)
+        rdma(mine, mine, send(1), recv(1), left)
+
+    def gather_relay(rows, send, recv):
+        arrived(rows(hl, 0, R), recv(0))
+        part = rows(hl, 0, R2)
+        rdma(part, part, send(2), recv(2), right)
+        arrived(rows(hr, 0, R), recv(1))
+        part = rows(hr, R2, R2)
+        rdma(part, part, send(3), recv(3), left)
+
+    def gather_end(rows, recv):
+        arrived(rows(ho, 0, R2), recv(2))
+        arrived(rows(ho, R2, R2), recv(3))
+
+    def scatter_start(tx, rb, send, recv):
+        rdma(tx.at[pl.ds(ho * R, R2), :], rb.at[0], send(0), recv(0), right)
+        rdma(tx.at[pl.ds(ho * R + R2, R2), :], rb.at[1], send(1), recv(1), left)
+
+    def scatter_relay(tx, rb, rx, send, recv):
+        arrived(rb.at[0], recv(0))
+        at = pl.ds(pl.multiple_of(hr * R, R2), R2)
+        tx[at, :] = (tx[at, :].astype(F32) + rb[0].astype(F32)).astype(BF16)
+        rdma(tx.at[pl.ds(hr * R, R), :], rx.at[0], send(2), recv(2), right)
+        arrived(rb.at[1], recv(1))
+        at = pl.ds(pl.multiple_of(hl * R + R2, R2), R2)
+        tx[at, :] = (tx[at, :].astype(F32) + rb[1].astype(F32)).astype(BF16)
+        rdma(tx.at[pl.ds(hl * R, R), :], rx.at[1], send(3), recv(3), left)
+
+    def scatter_end(tx, rx, recv):
+        arrived(rx.at[0], recv(2))
+        arrived(rx.at[1], recv(3))
+        own = tx[pl.ds(pl.multiple_of(h * R, R), R), :].astype(F32)
+        return own + rx[0].astype(F32) + rx[1].astype(F32)
 
     barrier = pltpu.get_barrier_semaphore()
     count = 0
@@ -99,12 +139,18 @@
         pltpu.make_async_copy(out_w, wo.at[c], loc_sem.at[3]),
         pltpu.make_async_copy(up_w, wu.at[c], loc_sem.at[4]),
         pltpu.make_async_copy(down_w, wd.at[c], loc_sem.at[5]),
+        pltpu.make_async_copy(cond, cond_v, loc_sem.at[6]),
+        pltpu.make_async_copy(q_gain, qg_v, loc_sem.at[7]),
+        pltpu.make_async_copy(k_gain, kg_v, loc_sem.at[8]),
     ]
     for copy in local:
         copy.start()
 
-    condf = cond[...].astype(F32)
-    active = (condf * jax.nn.sigmoid(condf)).astype(BF16)
+    cf[...] = jnp.zeros_like(cf)
+    local[6].wait()
+    condf = cond_v[...].astype(F32)
+    active = condf * jax.nn.sigmoid(condf)
+    active = jnp.concatenate([active[i:i + 1] for i in range(features // 128)], axis=1).astype(BF16)
     local[0].wait()
     share = lax.dot_general(
         jnp.broadcast_to(active, (16, features)), mw[...],
@@ -208,26 +254,32 @@
 
     local[2].wait()
     arrived(wq.at[:, 1 - c], w_recv.at[0])
+    def rs_sems(sems, g):
+        return lambda k: sems.at[g, k]
+
     for g in range(3):
         part = jnp.dot(n0, wq[g, 0], preferred_element_type=F32)
         part = part + jnp.dot(n1, wq[g, 1], preferred_element_type=F32)
         rs_tx[g] = part.astype(BF16)
-        for k in y_far:
-            hp, dev = y_peer(k)
-            rdma(rs_tx.at[g, pl.ds(hp * R, R), :], rs_rx.at[g, h], rs_send.at[g, k], rs_recv.at[g, h], dev)
-        rs_rx[g, h] = rs_tx[g, pl.ds(h * R, R), :]
-
-    slot = c * H + h
+        scatter_start(rs_tx.at[g], rs_rb.at[g], rs_sems(rs_send, g), rs_sems(rs_recv, g))
+
     heads = W // 128
-    for g in range(3):
-        for k in y_near:
-            hp, _ = y_peer(k)
-            arrived(rs_rx.at[g, hp], rs_recv.at[g, hp])
-        total = rs_rx[g, 0].astype(F32)
-        for hp in range(1, H):
-            total = total + rs_rx[g, hp].astype(F32)
+
+    def proj_relay(g):
+        scatter_relay(rs_tx.at[g], rs_rb.at[g], rs_rx.at[g], rs_sems(rs_send, g), rs_sems(rs_recv, g))
+
+    def kv_rows(g):
+        return lambda hp, lo, n: kv_rx.at[g, pl.ds((c * H + hp) * R + lo, n), :]
+
+    def to_mate(g, hp, i):
+        rows = kv_rows(g)(hp, 0, R)
+        rdma(rows, rows, km_send.at[g, i], km_recv.at[g, hp], mate)
+
+    def proj_end(g):
+        total = scatter_end(rs_tx.at[g], rs_rx.at[g], rs_sems(rs_recv, g))
         if g < 2:
-            gain = (q_gain if g == 0 else k_gain)[...]
+            local[7 + g].wait()
+            gain = (qg_v if g == 0 else kg_v)[...]
             pieces = []
             for hd in range(heads):
                 piece = total[:, 128 * hd:128 * (hd + 1)]
@@ -235,36 +287,41 @@
                 pieces.append(piece * lax.rsqrt(ms + 1e-06) * gain)
             total = jnp.concatenate(pieces, axis=1)
         if g == 0:
-            q_rx[pl.ds(b * R, R), :] = total.astype(BF16)
-            for k in range(1, B):
-                rows = q_rx.at[pl.ds(b * R, R), :]
+            rows = q_rx.at[pl.ds(b * R, R), :]
+            q_rx[pl.ds(pl.multiple_of(b * R, R), R), :] = total.astype(BF16)
+            for k in sorted(range(1, B), key=lambda k: -min(k, B - k)):
                 rdma(rows, rows, q_send.at[k], q_recv.at[b], {"blk": lax.rem(b + k, B)})
         else:
-            rows = kv_rx.at[g - 1, pl.ds(slot * R, R), :]
-            kv_rx[g - 1, pl.ds(slot * R, R), :] = total.astype(BF16)
-            for k in y_far:
-                _, dev = y_peer(k)
-                rdma(rows, rows, kv_send.at[g - 1, k], kv_recv.at[g - 1, slot], dev)
-            rdma(rows, rows, kv_send.at[g - 1, 0], kv_recv.at[g - 1, slot], mate)
+            kv_rx[g - 1, pl.ds(pl.multiple_of((c * H + h) * R, R), R), :] = total.astype(BF16)
+            gather_start(kv_rows(g - 1), rs_sems(kv_send, g - 1), rs_sems(kv_recv, g - 1))
+            to_mate(g - 1, h, 0)
+
+    proj_relay(0)
+    proj_relay(1)
+    proj_end(0)
+    proj_relay(2)
+    proj_end(1)
+    proj_end(2)
     for g in range(2):
-        for k in y_near:
-            hp, _ = y_peer(k)
-            sp = c * H + hp
-            rows = kv_rx.at[g, pl.ds(sp * R, R), :]
-            arrived(rows, kv_recv.at[g, sp])
-            rdma(rows, rows, kv_send.at[g, 4 + k], kv_recv.at[g, sp], mate)
+        gather_relay(kv_rows(g), rs_sems(kv_send, g), rs_sems(kv_recv, g))
+        to_mate(g, hl, 1)
+        to_mate(g, hr, 2)
+    for g in range(2):
+        gather_end(kv_rows(g), rs_sems(kv_recv, g))
+        to_mate(g, ho, 3)
     for k in range(1, B):
         bp = lax.rem(b + k, B)
         arrived(q_rx.at[pl.ds(bp * R, R), :], q_recv.at[bp])
     for g in range(2):
         for hp in range(H):
-            sp = (1 - c) * H + hp
-            arrived(kv_rx.at[g, pl.ds(sp * R, R), :], kv_recv.at[g, sp])
+            arrived(kv_rx.at[g, pl.ds(((1 - c) * H + hp) * R, R), :], km_recv.at[g, hp])
 
     scale = 1.0 / math.sqrt(128)
-    QB = 128 if B * R % 128 == 0 else R
-
-    def attend(qb, carry):
+    QB = 2 * R
+    nq = B // 2
+    rest = []
+    for i, off in enumerate(sorted(range(nq), key=lambda k: -min(k, nq - k))):
+        qb = lax.rem(b // 2 + off, nq)
         at = pl.multiple_of(qb * QB, QB)
         lane_q = lax.broadcasted_iota(jnp.int32, (QB, 128), 1)
         tail = jnp.zeros((QB, 128), F32)
@@ -274,51 +331,57 @@
                 q_rx[pl.ds(at, QB), cut], kv_rx[0, :, cut],
                 (((1,), (1,)), ((), ())), preferred_element_type=F32,
             )
-            top = jnp.max(s, axis=-1, keepdims=True).astype(BF16).astype(F32)
+            top = jnp.max(s, axis=-1, keepdims=True)
             p = jnp.exp((s - top) * scale)
             weight = jnp.sum(p, axis=-1, keepdims=True)
             o = jnp.dot(p.astype(BF16), kv_rx[1, :, cut], preferred_element_type=F32)
             o_tx[pl.ds(at, QB), cut] = o.astype(BF16)
-            high = weight.astype(BF16).astype(F32)
             tail = jnp.where(lane_q == hd, top, tail)
-            tail = jnp.where(lane_q == heads + hd, high, tail)
-            tail = jnp.where(lane_q == 2 * heads + hd, weight - high, tail)
-        o_tx[pl.ds(at, QB), W:W + 128] = tail.astype(BF16)
-        return carry
-
-    lax.fori_loop(0, B * R // QB, attend, 0)
-    o_rx[b] = o_tx[pl.ds(b * R, R), :]
-    for k in sorted(range(1, B), key=lambda k: -min(k, B - k)):
+            tail = jnp.where(lane_q == heads + hd, weight, tail)
+        os_tx[qb] = jnp.transpose(tail)[0:8]
+        targets = [2 * qb, 2 * qb + 1]
+        if off == 0:
+            o_rx[b] = o_tx[pl.ds(pl.multiple_of(b * R, R), R), :]
+            os_rx[b] = os_tx[qb]
+            targets = [b + 1 - 2 * lax.rem(b, 2)]
+        for e, bp in enumerate(targets):
+            dev = {"blk": bp}
+            rdma(o_tx.at[pl.ds(bp * R, R), :], o_rx.at[b], o_send.at[2 * i + e], o_recv.at[b], dev)
+            rdma(os_tx.at[qb], os_rx.at[b], os_send.at[2 * i + e], os_recv.at[b], dev)
+    for k in range(1, B):
         bp = lax.rem(b + k, B)
-        rdma(o_tx.at[pl.ds(bp * R, R), :], o_rx.at[b], o_send.at[k], o_recv.at[b], {"blk": bp})
+        arrived(os_rx.at[bp], os_recv.at[bp])
+    for hd in range(heads):
+        tops = [os_rx[bp, hd:hd + 1, :] for bp in range(B)]
+        top = functools.reduce(jnp.maximum, tops)
+        shares = [jnp.exp((tops[bp] - top) * scale) for bp in range(B)]
+        den = shares[0] * os_rx[0, heads + hd:heads + hd + 1, :]
+        for bp in range(1, B):
+            den = den + shares[bp] * os_rx[bp, heads + hd:heads + hd + 1, :]
+        for bp in range(B):
+            cf[hd * B + bp:hd * B + bp + 1, :] = shares[bp] / den
+    cf_t[...] = jnp.transpose(cf[...])
+    coef = cf_t[pl.ds(pl.multiple_of(lax.rem(b, 2) * R, R), R), :]
     for k in range(1, B):
         bp = lax.rem(b + k, B)
         arrived(o_rx.at[bp], o_recv.at[bp])
     pieces = []
     for hd in range(heads):
         cut = slice(128 * hd, 128 * (hd + 1))
-        tops = [o_rx[bp, :, W + hd:W + hd + 1].astype(F32) for bp in range(B)]
-        top = functools.reduce(jnp.maximum, tops)
-        num = jnp.zeros((R, 128), F32)
-        den = jnp.zeros((R, 1), F32)
-        for bp in range(B):
-            share_b = jnp.exp((tops[bp] - top) * scale)
-            num = num + share_b * o_rx[bp, :, cut].astype(F32)
-            den = den + share_b * (
-                o_rx[bp, :, W + heads + hd:W + heads + hd + 1].astype(F32)
-                + o_rx[bp, :, W + 2 * heads + hd:W + 2 * heads + hd + 1].astype(F32)
-            )
-        pieces.append(num / den)
-    mine = ctx_rx.at[pl.ds(h * R, R), :]
-    ctx_rx[pl.ds(h * R, R), :] = jnp.concatenate(pieces, axis=1).astype(BF16)
-    for k in y_far:
-        _, dev = y_peer(k)
-        rdma(mine, mine, cx_send.at[k], cx_recv.at[h], dev)
+        num = coef[:, hd * B:hd * B + 1] * o_rx[0, :, cut].astype(F32)
+        for bp in range(1, B):
+            num = num + coef[:, hd * B + bp:hd * B + bp + 1] * o_rx[bp, :, cut].astype(F32)
+        pieces.append(num)
+
+    def ctx_rows(hp, lo, n):
+        return ctx_rx.at[pl.ds(hp * R + lo, n), :]
+
+    ctx_rx[pl.ds(pl.multiple_of(h * R, R), R), :] = jnp.concatenate(pieces, axis=1).astype(BF16)
+    gather_start(ctx_rows, lambda k: cx_send.at[k], lambda k: cx_recv.at[k])
+    gather_relay(ctx_rows, lambda k: cx_send.at[k], lambda k: cx_recv.at[k])
     local[3].wait()
     arrived(wo.at[1 - c], w_recv.at[1])
-    for k in y_near:
-        hp, _ = y_peer(k)
-        arrived(ctx_rx.at[pl.ds(hp * R, R), :], cx_recv.at[hp])
+    gather_end(ctx_rows, lambda k: cx_recv.at[k])
 
     def to_owners(tx, rx, send, recv, cc):
         for hp in range(H):
@@ -381,37 +444,47 @@
             arrived(n2_rx.at[cc, pl.ds(i * R, R), :], n2_recv.at[cc, i])
 
     J = up_w.shape[1] // W
+
+    def act_rows(j):
+        return lambda hp, lo, n: act_rx.at[j, pl.ds(hp * R + lo, n), :]
+
     for j in range(J):
         cut = slice(W * j, W * (j + 1))
         part = jnp.dot(n2_rx[0], wu[0, :, cut], preferred_element_type=F32)
         part = part + jnp.dot(n2_rx[1], wu[1, :, cut], preferred_element_type=F32)
         up_tx[j] = part.astype(BF16)
-        for k in y_far:
-            hp, dev = y_peer(k)
-            rdma(up_tx.at[j, pl.ds(hp * R, R), :], up_rx.at[j, h], up_send.at[j, k], up_recv.at[j, h], dev)
-        up_rx[j, h] = up_tx[j, pl.ds(h * R, R), :]
-    for j in range(J):
-        for k in y_near:
-            hp, _ = y_peer(k)
-            arrived(up_rx.at[j, hp], up_recv.at[j, hp])
-        hidden = up_rx[j, 0].astype(F32)
-        for hp in range(1, H):
-            hidden = hidden + up_rx[j, hp].astype(F32)
-        mine = act_rx.at[j, pl.ds(h * R, R), :]
-        act_rx[j, pl.ds(h * R, R), :] = jax.nn.gelu(hidden, approximate=True).astype(BF16)
-        for k in y_far:
-            _, dev = y_peer(k)
-            rdma(mine, mine, ac_send.at[j, k], ac_recv.at[j, h], dev)
-    local[5].wait()
-    arrived(wd.at[1 - c], w_recv.at[3])
+        scatter_start(up_tx.at[j], up_rb.at[j], rs_sems(up_send, j), rs_sems(up_recv, j))
+
+    def ff_relay(j):
+        scatter_relay(up_tx.at[j], up_rb.at[j], up_rx.at[j], rs_sems(up_send, j), rs_sems(up_recv, j))
+
+    def ff_end(j):
+        hidden = scatter_end(up_tx.at[j], up_rx.at[j], rs_sems(up_recv, j))
+        act_rx[j, pl.ds(pl.multiple_of(h * R, R), R), :] = jax.nn.gelu(hidden, approximate=True).astype(BF16)
+        gather_start(act_rows(j), rs_sems(ac_send, j), rs_sems(ac_recv, j))
+
+    def act_relay(j):
+        gather_relay(act_rows(j), rs_sems(ac_send, j), rs_sems(ac_recv, j))
+
     accs = [None] * C
-    for j in range(J):
-        for k in y_near:
-            hp, _ = y_peer(k)
-            arrived(act_rx.at[j, pl.ds(hp * R, R), :], ac_recv.at[j, hp])
+
+    def act_end(j):
+        gather_end(act_rows(j), rs_sems(ac_recv, j))
         for cc in range(C):
             part = jnp.dot(act_rx[j], wd[cc, W * j:W * (j + 1), :], preferred_element_type=F32)
             accs[cc] = part if j == 0 else accs[cc] + part
+
+    steps = []
+    for j in range(J):
+        for n, step in enumerate((ff_relay, ff_end, act_relay, act_end)):
+            steps.append((j + 1.5 * n, n, j, step))
+    waited = False
+    for _, n, j, step in sorted(steps, key=lambda item: item[:3]):
+        if n == 3 and not waited:
+            local[5].wait()
+            arrived(wd.at[1 - c], w_recv.at[3])
+            waited = True
+        step(j)
     for cc in range(C):
         ff_tx[cc] = accs[cc].astype(BF16)
         to_owners(ff_tx, ff_rx, ff_send, ff_recv, cc)
@@ -442,15 +515,18 @@
     J = FFL // W
     dma = pltpu.SemaphoreType.DMA
     vmem = pltpu.VMEM
-    any_spec = pl.BlockSpec(memory_space=pl.ANY)
+    any_spec = pl.BlockSpec(memory_space=pltpu.HBM)
     vm_spec = pl.BlockSpec(memory_space=pltpu.VMEM)
     return pl.pallas_call(
         functools.partial(block_kernel, U, B, T),
         out_shape=jax.ShapeDtypeStruct((R, W), F32),
-        in_specs=[any_spec, vm_spec, any_spec, any_spec, vm_spec, vm_spec, any_spec, any_spec, any_spec],
+        in_specs=[any_spec] * 9,
         out_specs=vm_spec,
         scratch_shapes=[
             vmem((R, W), BF16),
+            vmem((mod_weight.shape[0] // 128, 128), BF16),
+            vmem((1, 128), F32),
+            vmem((1, 128), F32),
             vmem((2, G, W), BF16),
             vmem((mod_weight.shape[1], mod_weight.shape[0]), BF16),
             vmem((3, 2, W, W), BF16),
@@ -467,11 +543,16 @@
             vmem((8, G), F32),
             vmem((H, 8, G), F32),
             vmem((3, G, W), BF16),
-            vmem((3, H, R, W), BF16),
+            vmem((3, 2, R // 2, W), BF16),
+            vmem((3, 2, R, W), BF16),
             vmem((B * R, W), BF16),
             vmem((2, T * R, W), BF16),
-            vmem((B * R, W + 128), BF16),
-            vmem((B, R, W + 128), BF16),
+            vmem((B * R, W), BF16),
+            vmem((B, R, W), BF16),
+            vmem((B // 2, 8, 128), F32),
+            vmem((B, 8, 128), F32),
+            vmem((128, 128), F32),
+            vmem((128, 128), F32),
             vmem((G, W), BF16),
             vmem((2, G, W), BF16),
             vmem((U, R, W), BF16),
@@ -481,23 +562,24 @@
             vmem((R, W), BF16),
             vmem((2, G, W), BF16),
             vmem((J, G, W), BF16),
-            vmem((J, H, R, W), BF16),
+            vmem((J, 2, R // 2, W), BF16),
+            vmem((J, 2, R, W), BF16),
             vmem((J, G, W), BF16),
             vmem((2, G, W), BF16),
             vmem((U, R, W), BF16),
-            dma((6,)), dma((4,)), dma((4,)),
+            dma((9,)), dma((4,)), dma((4,)),
             dma((U,)), dma((2, H)), dma((B,)), dma((B,)), dma((T,)), dma((T,)), dma((U,)), dma((U,)),
-            dma((H,)), dma((H,)), dma((3, H)), dma((3, H)), dma((B,)), dma((B,)), dma((2, 8)), dma((2, T)), dma((B,)), dma((B,)),
+            dma((H,)), dma((H,)), dma((3, H)), dma((3, H)), dma((B,)), dma((B,)), dma((2, H)), dma((2, H)), dma((2, H)), dma((2, H)), dma((B,)), dma((B,)), dma((B,)), dma((B,)),
             dma((H,)), dma((H,)), dma((2, H)), dma((U,)), dma((T,)), dma((T,)), dma((U,)), dma((2, H)),
             dma((J, H)), dma((J, H)), dma((J, H)), dma((J, H)), dma((2, H)), dma((U,)),
         ],
         compiler_params=pltpu.CompilerParams(
-            collective_id=0, has_side_effects=True, vmem_limit_bytes=48 * 1024 * 1024
+            collective_id=0, has_side_effects=True, vmem_limit_bytes=67043328
         ),
         name="block_kernel",
     )(
         tokens,
-        cond.reshape(1, -1),
+        cond.reshape(-1, 128),
         mod_weight.T,
         qkv_weight.transpose(1, 0, 2),
         q_gain.reshape(1, -1),

time: 155 us -> 137 us (0.88)
  Pallas kernels: 145 us -> 135 us
  local copies, waits for them, and re-layouts: 9.06 us -> 1.54 us
    pallas_call x1, Pallas kernels: 145 us -> 135 us  [on_device(): pl.pallas_call(functools.partial(block_kernel, U, B, T), out_shape=jax.Sh...]
    unnamed x17 -> x1, local copies, waits for them, and re-layouts: 8.36 us -> 1.54 us
where the time goes in v2:
time: 137 us
  Pallas kernels  135 us (99%)
  local copies, waits for them, and re-layouts  1.54 us (1%)
    pallas_call x1, Pallas kernels, on_device(): pl.pallas_call(functools.partial(block_kernel, U, B, T), out_shape=jax.Sh...  135 us

profile of v2, /device:TPU:1, one launch (start us, length us, event | category | flops | bytes accessed | tf_op | source)
XLA Modules:
  0.0 136.7 jit_solution(8908875907812351014)
XLA Ops:
  0.0 135.1 %block_kernel.1 = f32[64,384]{1,0:T(8,128)} custom-call(bf16[64,384]{1,0:T(8,128)(2,1)} %tokens.1, bf16[24,128]{1,0:T(8,128)(2,1)} %bitcast.7, bf16[36,3072]{1,0:T(8,128)(2,1)} %bitcast.6, bf16[3,384,384]{2,1,0:T(8,128)(2,1)} %bitcast.5, f32[1,128]{1,0:T(1,128)} %bitcast.8, f32[1,128]{1,0:T(1,128)} %bitcast.9, bf16[384,384]{1,0:T(8,128)(2,1)} %out_w.1, ...), custom_call_target="tpu_custom_call" | custom-call | tf_op jit(solution)/shard_map/block_kernel/pallas_call | solution.py:520
  135.1 1.5 %copy.11 = f32[64,384]{1,0:T(8,128)} copy(f32[64,384]{1,0:T(8,128)} %block_kernel.1) | data formatting | bytes 196608

commit v3 on v2

v3 whole, which is shorter than its diff:
```python
import functools
import math

import jax
import jax.numpy as jnp
from jax import lax
from jax.experimental import pallas as pl
from jax.experimental.pallas import tpu as pltpu
from jax.sharding import PartitionSpec as P

ORDER = [int(s) for s in "01001010101001010011010101011101"]
MESH = pl.DeviceIdType.MESH
F32 = jnp.float32
BF16 = jnp.bfloat16


def block_kernel(
    U, B, T,
    tokens, cond, mod_w, qkv_w, q_gain, k_gain, out_w, up_w, down_w,
    out,
    tok_own, cond_v, qg_v, kg_v, tok_rx, mw, wq, wo, wu, wd,
    m_tx, m_a, m_d, m_b, m_u, m_c, modv,
    st_tx, st_rx, rs_tx, rs_rb, rs_rx, q_rx, kv_rx, o_tx, o_rx, os_tx, os_rx, cf, cf_t, ctx_rx,
    at_tx, at_rx, mix, s2_tx, s2_rx, fx_tx, fx_rx, cv_tx, cv_rx, n2_tx, n2_rx, up_tx, up_rb, up_rx, act_rx, ff_tx, ff_rx,
    loc_sem, w_send, w_recv,
    tok_send, tok_recv, ma_send, ma_recv, mb_send, mb_recv, mc_send, mc_recv,
    st_send, st_recv, rs_send, rs_recv, q_send, q_recv, kv_send, kv_recv, km_send, km_recv, o_send, o_recv, os_send, os_recv,
    cx_send, cx_recv, at_send, at_recv, s2_send, s2_recv, fx_send, fx_recv, cv_send, cv_recv, n2_send, n2_recv,
    up_send, up_recv, ac_send, ac_recv, ff_send, ff_recv,
):
    C = 2
    H = T // C
    R, W = tokens.shape
    G = H * R
    S = 2
    N = R // S
    GN = H * N
    features = W * T
    u = lax.axis_index("ulysses")
    b = lax.axis_index("blk")
    t = lax.axis_index("tensor")
    h = t // C
    c = lax.rem(t, C)
    mate = {"tensor": h * C + (1 - c)}
    uc = u // H
    ui = lax.rem(u, H)
    pending = []

    def rdma(src, dst, send, recv, dev):
        copy = pltpu.make_async_remote_copy(
            src_ref=src, dst_ref=dst, send_sem=send, recv_sem=recv,
            device_id=dev, device_id_type=MESH,
        )
        copy.start()
        pending.append((None, copy))

    def rdma_or_local(own, src, dst, send, recv, dev):
        copy = pltpu.make_async_remote_copy(
            src_ref=src, dst_ref=dst, send_sem=send, recv_sem=recv,
            device_id=dev, device_id_type=MESH,
        )

        @pl.when(own)
        def _():
            pltpu.make_async_copy(src, dst, recv).start()

        @pl.when(jnp.logical_not(own))
        def _():
            copy.start()

        pending.append((own, copy))

    def arrived(dst, recv):
        pltpu.make_async_copy(dst, dst, recv).wait()

    def y_peer(k):
        hp = lax.rem(h + k, H)
        return hp, {"tensor": hp * C + c}

    hr, right = y_peer(1)
    ho, _ = y_peer(2)
    hl, left = y_peer(3)

    def gather_start(rows, n, send, recv):
        mine = rows(h, 0, n)
        rdma(mine, mine, send(0), recv(0), right)
        rdma(mine, mine, send(1), recv(1), left)

    def gather_relay(rows, n, send, recv):
        half = n // 2
        arrived(rows(hl, 0, n), recv(0))
        part = rows(hl, 0, half)
        rdma(part, part, send(2), recv(2), right)
        arrived(rows(hr, 0, n), recv(1))
        part = rows(hr, half, half)
        rdma(part, part, send(3), recv(3), left)

    def gather_end(rows, n, recv):
        half = n // 2
        arrived(rows(ho, 0, half), recv(2))
        arrived(rows(ho, half, half), recv(3))

    def scatter_start(tx, rb, n, send, recv):
        half = n // 2
        rdma(tx.at[pl.ds(ho * n, half), :], rb.at[0], send(0), recv(0), right)
        rdma(tx.at[pl.ds(ho * n + half, half), :], rb.at[1], send(1), recv(1), left)

    def scatter_relay(tx, rb, rx, n, send, recv):
        half = n // 2
        for side, (to, dev) in enumerate(((hr, right), (hl, left))):
            arrived(rb.at[side], recv(side))
            at = pl.ds(pl.multiple_of(to * n + side * half, half), half)
            tx[at, :] = (tx[at, :].astype(F32) + rb[side].astype(F32)).astype(BF16)
            rdma(tx.at[pl.ds(to * n, n), :], rx.at[side], send(2 + side), recv(2 + side), dev)

    def scatter_end(tx, rx, n, recv):
        arrived(rx.at[0], recv(2))
        arrived(rx.at[1], recv(3))
        own = tx[pl.ds(pl.multiple_of(h * n, n), n), :].astype(F32)
        return own + rx[0].astype(F32) + rx[1].astype(F32)

    barrier = pltpu.get_barrier_semaphore()
    count = 0
    for k in range(1, B):
        pl.semaphore_signal(barrier, inc=1, device_id={"blk": lax.rem(b + k, B)}, device_id_type=MESH)
        count += 1
    for k in range(1, T):
        pl.semaphore_signal(barrier, inc=1, device_id={"tensor": lax.rem(t + k, T)}, device_id_type=MESH)
        count += 1
    for k in range(1, U):
        for cc in range(C):
            pl.semaphore_signal(
                barrier, inc=1,
                device_id={"ulysses": lax.rem(u + k, U), "tensor": h * C + cc},
                device_id_type=MESH,
            )
            count += 1

    local = [
        pltpu.make_async_copy(mod_w, mw, loc_sem.at[0]),
        pltpu.make_async_copy(tokens, tok_own, loc_sem.at[1]),
        pltpu.make_async_copy(qkv_w, wq.at[:, c], loc_sem.at[2]),
        pltpu.make_async_copy(out_w, wo.at[c], loc_sem.at[3]),
        pltpu.make_async_copy(up_w, wu.at[c], loc_sem.at[4]),
        pltpu.make_async_copy(down_w, wd.at[c], loc_sem.at[5]),
        pltpu.make_async_copy(cond, cond_v, loc_sem.at[6]),
        pltpu.make_async_copy(q_gain, qg_v, loc_sem.at[7]),
        pltpu.make_async_copy(k_gain, kg_v, loc_sem.at[8]),
    ]
    for copy in local:
        copy.start()

    cf[...] = jnp.zeros_like(cf)
    local[6].wait()
    condf = cond_v[...].astype(F32)
    active = condf * jax.nn.sigmoid(condf)
    active = jnp.concatenate([active[i:i + 1] for i in range(features // 128)], axis=1).astype(BF16)
    local[0].wait()
    share = lax.dot_general(
        jnp.broadcast_to(active, (16, features)), mw[...],
        (((1,), (1,)), ((), ())), preferred_element_type=F32,
    )
    n_share = mod_w.shape[0]
    start = n_share * (b * T + t)
    lanes2 = lax.broadcasted_iota(jnp.int32, (n_share, 256), 1)
    rows2 = lax.broadcasted_iota(jnp.int32, (n_share, 256), 0)
    place = (lanes2 == rows2 + lax.rem(start, 128)).astype(F32)
    placed = jnp.dot(share[0:8], place, preferred_element_type=F32, precision=lax.Precision.HIGHEST)
    sub8 = lax.broadcasted_iota(jnp.int32, (8, 128), 0)
    tile = jnp.where(sub8 == 0, placed[:, 0:128], jnp.where(sub8 == 1, placed[:, 128:256], 0.0))
    m_tx[...] = tile
    m_a[b] = tile

    pl.semaphore_wait(barrier, count)

    for k in range(1, B):
        rdma(m_tx, m_a.at[b], ma_send.at[k], ma_recv.at[b], {"blk": lax.rem(b + k, B)})
    for up_ in range(U):
        rdma_or_local(
            jnp.logical_and(u == up_, c == uc),
            tokens, tok_rx.at[c, pl.ds(ui * R, R), :], tok_send.at[up_], tok_recv.at[c, ui],
            {"ulysses": up_, "tensor": h * C + uc},
        )
    rdma(qkv_w, wq.at[:, c], w_send.at[0], w_recv.at[0], mate)
    rdma(out_w, wo.at[c], w_send.at[1], w_recv.at[1], mate)
    rdma(up_w, wu.at[c], w_send.at[2], w_recv.at[2], mate)
    rdma(down_w, wd.at[c], w_send.at[3], w_recv.at[3], mate)

    per_u = n_share * B * T // 128
    m_d[...] = jnp.zeros_like(m_d)
    for k in range(B):
        if k:
            bp = lax.rem(b + k, B)
            arrived(m_a.at[bp], ma_recv.at[bp])
    for bp in range(B):
        row = (n_share * (bp * T + t)) // 128
        m_d[pl.ds(row, 1), :] += m_a[bp, 0:1, :]
        m_d[pl.ds(row + 1, 1), :] += m_a[bp, 1:2, :]
    m_b[t] = m_d[...]
    for k in range(1, T):
        rdma(m_d, m_b.at[t], mb_send.at[k], mb_recv.at[t], {"tensor": lax.rem(t + k, T)})

    for cc in range(C):
        for i in range(H):
            arrived(tok_rx.at[cc, pl.ds(i * R, R), :], tok_recv.at[cc, i])
    x0 = tok_rx[0].astype(F32)
    x1 = tok_rx[1].astype(F32)
    local_mean = (jnp.sum(x0, -1, keepdims=True) + jnp.sum(x1, -1, keepdims=True)) * (1.0 / (C * W))
    d0 = x0 - local_mean
    d1 = x1 - local_mean
    local_m2 = jnp.sum(d0 * d0, -1, keepdims=True) + jnp.sum(d1 * d1, -1, keepdims=True)
    lane = lax.broadcasted_iota(jnp.int32, (G, 128), 1)
    stats = jnp.where(lane == 0, local_mean, jnp.where(lane == 1, local_m2, 0.0))
    stats_t = jnp.transpose(stats)[0:8]
    st_tx[...] = stats_t
    st_rx[h] = stats_t
    for k in range(1, H):
        hp, dev = y_peer(k)
        rdma(st_tx, st_rx.at[h], st_send.at[k], st_recv.at[h], dev)

    for k in range(1, T):
        tp = lax.rem(t + k, T)
        arrived(m_b.at[tp], mb_recv.at[tp])
    dense = m_b[0]
    for tp in range(1, T):
        dense = dense + m_b[tp]
    m_u[...] = dense
    m_c[u] = dense
    for k in range(1, U):
        rdma(m_u, m_c.at[u], mc_send.at[k], mc_recv.at[u], {"ulysses": lax.rem(u + k, U)})

    for k in range(1, H):
        hp, _ = y_peer(k)
        arrived(st_rx.at[hp], st_recv.at[hp])
    mean = st_rx[0, 0:1, :]
    for hp in range(1, H):
        mean = mean + st_rx[hp, 0:1, :]
    mean = mean * (1.0 / H)
    m2 = jnp.zeros_like(mean)
    for hp in range(H):
        diff = st_rx[hp, 0:1, :] - mean
        m2 = m2 + st_rx[hp, 1:2, :] + (C * W) * diff * diff
    rstd = lax.rsqrt(m2 * (1.0 / features) + 1e-06)
    subg = lax.broadcasted_iota(jnp.int32, (128, G), 0)
    cols = jnp.transpose(jnp.where(subg == 0, mean, jnp.where(subg == 1, rstd, 0.0)))
    mean_c, rstd_c = cols[:, 0:1], cols[:, 1:2]

    for k in range(1, U):
        upk = lax.rem(u + k, U)
        arrived(m_c.at[upk], mc_recv.at[upk])
    for v in range(6):
        for k in range(C * W // 128):
            row = v * (features // 128) + h * (C * W // 128) + k
            modv[v:v + 1, 128 * k:128 * (k + 1)] = m_c[row // per_u, pl.ds(lax.rem(row, per_u), 1), :]

    n0 = ((x0 - mean_c) * rstd_c * (1.0 + modv[1:2, 0:W]) + modv[0:1, 0:W]).astype(BF16)
    n1 = ((x1 - mean_c) * rstd_c * (1.0 + modv[1:2, W:2 * W]) + modv[0:1, W:2 * W]).astype(BF16)

    local[2].wait()
    arrived(wq.at[:, 1 - c], w_recv.at[0])
    def rs_sems(sems, g):
        return lambda k: sems.at[g, k]

    for g in range(3):
        part = jnp.dot(n0, wq[g, 0], preferred_element_type=F32)
        part = part + jnp.dot(n1, wq[g, 1], preferred_element_type=F32)
        rs_tx[g] = part.astype(BF16)
        scatter_start(rs_tx.at[g], rs_rb.at[g], R, rs_sems(rs_send, g), rs_sems(rs_recv, g))

    heads = W // 128

    def proj_relay(g):
        scatter_relay(rs_tx.at[g], rs_rb.at[g], rs_rx.at[g], R, rs_sems(rs_send, g), rs_sems(rs_recv, g))

    def kv_rows(g):
        return lambda hp, lo, n: kv_rx.at[g, pl.ds((c * H + hp) * R + lo, n), :]

    def to_mate(g, hp, i):
        rows = kv_rows(g)(hp, 0, R)
        rdma(rows, rows, km_send.at[g, i], km_recv.at[g, hp], mate)

    def proj_end(g):
        total = scatter_end(rs_tx.at[g], rs_rx.at[g], R, rs_sems(rs_recv, g))
        if g < 2:
            local[7 + g].wait()
            gain = (qg_v if g == 0 else kg_v)[...]
            pieces = []
            for hd in range(heads):
                piece = total[:, 128 * hd:128 * (hd + 1)]
                ms = jnp.mean(piece * piece, axis=-1, keepdims=True)
                pieces.append(piece * lax.rsqrt(ms + 1e-06) * gain)
            total = jnp.concatenate(pieces, axis=1)
        if g == 0:
            for s in range(S):
                q_rx[s, pl.ds(pl.multiple_of(b * N, N), N), :] = total[s * N:(s + 1) * N].astype(BF16)
                rows = q_rx.at[s, pl.ds(b * N, N), :]
                for k in sorted(range(1, B), key=lambda k: -min(k, B - k)):
                    rdma(rows, rows, q_send.at[s, k], q_recv.at[s, b], {"blk": lax.rem(b + k, B)})
        else:
            kv_rx[g - 1, pl.ds(pl.multiple_of((c * H + h) * R, R), R), :] = total.astype(BF16)
            gather_start(kv_rows(g - 1), R, rs_sems(kv_send, g - 1), rs_sems(kv_recv, g - 1))
            to_mate(g - 1, h, 0)

    local[4].wait()
    arrived(wu.at[1 - c], w_recv.at[2])
    for cc in range(C):
        cut = slice(cc * W, (cc + 1) * W)
        vecs = []
        for vec in (1.0 + modv[4:5, cut], modv[3:4, cut]):
            high = vec.astype(BF16).astype(F32)
            vecs += [high, vec - high]
        sub16 = lax.broadcasted_iota(jnp.int32, (16, W), 0)
        left_side = jnp.zeros((16, W), F32)
        for i, vec in enumerate(vecs):
            left_side = jnp.where(sub16 == i, vec, left_side)
        cols16 = jnp.dot(left_side.astype(BF16), wu[cc], preferred_element_type=F32)
        cv_tx[cc:cc + 1, :] = cols16[0:1] + cols16[1:2]
        shifted = cols16[2:3] + cols16[3:4]
        cv_tx[2:3, :] = shifted if cc == 0 else cv_tx[2:3, :] + shifted
    cv_tx[3:8, :] = jnp.zeros((5, wu.shape[2]), F32)
    cv_rx[h] = cv_tx[...]

    proj_relay(0)
    proj_relay(1)
    proj_end(0)
    proj_relay(2)
    proj_end(1)
    proj_end(2)
    for g in range(2):
        gather_relay(kv_rows(g), R, rs_sems(kv_send, g), rs_sems(kv_recv, g))
        to_mate(g, hl, 1)
        to_mate(g, hr, 2)
    for g in range(2):
        gather_end(kv_rows(g), R, rs_sems(kv_recv, g))
        to_mate(g, ho, 3)
    for k in range(1, B):
        bp = lax.rem(b + k, B)
        for s in range(S):
            arrived(q_rx.at[s, pl.ds(bp * N, N), :], q_recv.at[s, bp])
    for g in range(2):
        for hp in range(H):
            arrived(kv_rx.at[g, pl.ds(((1 - c) * H + hp) * R, R), :], km_recv.at[g, hp])

    scale = 1.0 / math.sqrt(128)
    TB = 128 // N
    nq = B // TB
    own_cols = pl.ds(pl.multiple_of(c * W, 128), W)
    J, FW = up_tx.shape[1], up_tx.shape[3]

    def sems(ref, *index):
        return lambda k: ref.at[(*index, k)]

    def to_owners(s, tx, rx, send, recv, cc):
        for hp in range(H):
            up_ = c * H + hp
            rdma_or_local(
                jnp.logical_and(up_ == u, c == cc),
                tx.at[s, cc, pl.ds(hp * N, N), :], rx.at[s, u], send.at[s, cc, hp], recv.at[s, u],
                {"ulysses": up_, "tensor": h * C + cc},
            )

    def from_owners(s, rx, recv):
        for up_ in range(U):
            arrived(rx.at[s, up_], recv.at[s, up_])
        total = rx[s, 0].astype(F32)
        for up_ in range(1, U):
            total = total + rx[s, up_].astype(F32)
        return total

    def fix_copies(s):
        return [
            pltpu.make_async_remote_copy(
                src_ref=fx_tx.at[s], dst_ref=fx_rx.at[s], send_sem=fx_send.at[s, k], recv_sem=fx_recv.at[s],
                device_id={"ulysses": lax.rem(u + k, U)}, device_id_type=MESH,
            )
            for k in range(1, U)
        ]

    def part_steps(s):
        for off in range(nq - 1, -1, -1):
            qb = lax.rem(b // TB + off, nq)
            at = pl.multiple_of(qb * 128, 128)
            lane_q = lax.broadcasted_iota(jnp.int32, (128, 128), 1)
            tail = jnp.zeros((128, 128), F32)
            for hd in range(heads):
                cut = slice(128 * hd, 128 * (hd + 1))
                score = lax.dot_general(
                    q_rx[s, pl.ds(at, 128), cut], kv_rx[0, :, cut],
                    (((1,), (1,)), ((), ())), preferred_element_type=F32,
                )
                top = jnp.max(score, axis=-1, keepdims=True)
                p = jnp.exp((score - top) * scale)
                weight = jnp.sum(p, axis=-1, keepdims=True)
                o = jnp.dot(p.astype(BF16), kv_rx[1, :, cut], preferred_element_type=F32)
                o_tx[s, pl.ds(at, 128), cut] = o.astype(BF16)
                tail = jnp.where(lane_q == hd, top, tail)
                tail = jnp.where(lane_q == heads + hd, weight, tail)
            os_tx[s, qb] = jnp.transpose(tail)[0:8]
            for e in range(TB):
                bp = TB * qb + lax.rem(b + e, TB)
                if off == 0 and e == 0:
                    o_rx[s, b] = o_tx[s, pl.ds(pl.multiple_of(b * N, N), N), :]
                    os_rx[s, b] = os_tx[s, qb]
                    continue
                k, dev = off * TB + e, {"blk": bp}
                rdma(o_tx.at[s, pl.ds(bp * N, N), :], o_rx.at[s, b], o_send.at[s, k], o_recv.at[s, b], dev)
                rdma(os_tx.at[s, qb], os_rx.at[s, b], os_send.at[s, k], os_recv.at[s, b], dev)
        yield

        if s == 0:
            for k in range(1, H):
                _, dev = y_peer(k)
                rdma(cv_tx, cv_rx.at[h], cv_send.at[k], cv_recv.at[h], dev)

        for k in range(1, B):
            bp = lax.rem(b + k, B)
            arrived(os_rx.at[s, bp], os_recv.at[s, bp])
        for hd in range(heads):
            tops = [os_rx[s, bp, hd:hd + 1, :] for bp in range(B)]
            top = functools.reduce(jnp.maximum, tops)
            shares = [jnp.exp((tops[bp] - top) * scale) for bp in range(B)]
            den = shares[0] * os_rx[s, 0, heads + hd:heads + hd + 1, :]
            for bp in range(1, B):
                den = den + shares[bp] * os_rx[s, bp, heads + hd:heads + hd + 1, :]
            for bp in range(B):
                cf[hd * B + bp:hd * B + bp + 1, :] = shares[bp] / den
        cf_t[...] = jnp.transpose(cf[...])
        coef = cf_t[pl.ds(pl.multiple_of(lax.rem(b, TB) * N, N), N), :]
        for k in range(1, B):
            bp = lax.rem(b + k, B)
            arrived(o_rx.at[s, bp], o_recv.at[s, bp])
        pieces = []
        for hd in range(heads):
            cut = slice(128 * hd, 128 * (hd + 1))
            num = coef[:, hd * B:hd * B + 1] * o_rx[s, 0, :, cut].astype(F32)
            for bp in range(1, B):
                num = num + coef[:, hd * B + bp:hd * B + bp + 1] * o_rx[s, bp, :, cut].astype(F32)
            pieces.append(num)

        def ctx_rows(hp, lo, n):
            return ctx_rx.at[s, pl.ds(hp * N + lo, n), :]

        ctx_rx[s, pl.ds(pl.multiple_of(h * N, N), N), :] = jnp.concatenate(pieces, axis=1).astype(BF16)
        gather_start(ctx_rows, N, sems(cx_send, s), sems(cx_recv, s))
        yield
        gather_relay(ctx_rows, N, sems(cx_send, s), sems(cx_recv, s))
        yield
        if s == 0:
            local[3].wait()
            arrived(wo.at[1 - c], w_recv.at[1])
        gather_end(ctx_rows, N, sems(cx_recv, s))

        for cc in range(C):
            at_tx[s, cc] = jnp.dot(ctx_rx[s], wo[cc], preferred_element_type=F32).astype(BF16)
            to_owners(s, at_tx, at_rx, at_send, at_recv, cc)
        yield
        attended = from_owners(s, at_rx, at_recv)
        if s == 0:
            local[1].wait()
        mine = slice(s * N, (s + 1) * N)
        mix[mine, :] = tok_own[mine, :].astype(F32) + modv[2:3, own_cols] * attended
        mixed = mix[mine, :]

        mean_l = jnp.sum(mixed, -1, keepdims=True) * (1.0 / W)
        diff = mixed - mean_l
        n2_tx[s] = (diff * (1.0 + modv[4:5, own_cols])).astype(BF16)
        for up_ in range(U):
            rdma_or_local(
                jnp.logical_and(u == up_, c == uc),
                n2_tx.at[s], n2_rx.at[s, c, pl.ds(ui * N, N), :], n2_send.at[s, up_], n2_recv.at[s, c, ui],
                {"ulysses": up_, "tensor": h * C + uc},
            )
        m2_l = jnp.sum(diff * diff, -1, keepdims=True)
        lane_r = lax.broadcasted_iota(jnp.int32, (N, 128), 1)
        st2 = jnp.where(lane_r == 0, mean_l, jnp.where(lane_r == 1, m2_l, 0.0))
        st2_t = jnp.transpose(jnp.concatenate([st2, jnp.zeros((128 - N, 128), F32)], axis=0))[0:8]
        s2_tx[s] = st2_t
        s2_rx[s, t] = st2_t
        for k in range(1, T):
            rdma(s2_tx.at[s], s2_rx.at[s, t], s2_send.at[s, k], s2_recv.at[s, t], {"tensor": lax.rem(t + k, T)})
        yield
        for cc in range(C):
            for i in range(H):
                arrived(n2_rx.at[s, cc, pl.ds(i * N, N), :], n2_recv.at[s, cc, i])

        def act_rows(j):
            return lambda hp, lo, n: act_rx.at[s, j, pl.ds(hp * N + lo, n), :]

        for j in range(J):
            cut = slice(FW * j, FW * (j + 1))
            part = jnp.dot(n2_rx[s, 0], wu[0, :, cut], preferred_element_type=F32)
            part = part + jnp.dot(n2_rx[s, 1], wu[1, :, cut], preferred_element_type=F32)
            up_tx[s, j] = part.astype(BF16)
            scatter_start(up_tx.at[s, j], up_rb.at[s, j], N, sems(up_send, s, j), sems(up_recv, s, j))
        yield
        for k in range(1, T):
            tp = lax.rem(t + k, T)
            arrived(s2_rx.at[s, tp], s2_recv.at[s, tp])
        total = s2_rx[s, 0]
        for tp in range(1, T):
            total = total + s2_rx[s, tp]
        mean2 = total[0:1] * (1.0 / T)
        m2 = total[1:2]
        for tp in range(T):
            dev2 = s2_rx[s, tp, 0:1, :] - mean2
            m2 = m2 + W * dev2 * dev2
            fx_tx[s, tp:tp + 1, :] = dev2
        fx_tx[s, T:T + 1, :] = lax.rsqrt(m2 * (1.0 / features) + 1e-06)
        fx_tx[s, T + 1:16, :] = jnp.zeros((16 - T - 1, 128), F32)
        sends = u == c * H + h

        @pl.when(sends)
        def _():
            fx_rx[s] = fx_tx[s]
            for copy in fix_copies(s):
                copy.start()

        yield
        for j in range(J):
            scatter_relay(
                up_tx.at[s, j], up_rb.at[s, j], up_rx.at[s, j], N, sems(up_send, s, j), sems(up_recv, s, j)
            )
            yield
        for j in range(J):
            hidden = scatter_end(up_tx.at[s, j], up_rx.at[s, j], N, sems(up_recv, s, j))
            if j == 0:

                @pl.when(u != c * H + h)
                def _():
                    arrived(fx_rx.at[s], fx_recv.at[s])

                if s == 0:
                    for k in range(1, H):
                        hp, _ = y_peer(k)
                        arrived(cv_rx.at[hp], cv_recv.at[hp])
                fix = jnp.transpose(jnp.concatenate([fx_rx[s], jnp.zeros((112, 128), F32)], axis=0))[0:N]
            cut = slice(FW * j, FW * (j + 1))
            shifted = cv_rx[0, 2:3, cut]
            for hp in range(1, H):
                shifted = shifted + cv_rx[hp, 2:3, cut]
            for tp in range(T):
                hidden = hidden + fix[:, tp:tp + 1] * cv_rx[tp // C, tp % C:tp % C + 1, cut]
            hidden = fix[:, T:T + 1] * hidden + shifted
            act_rx[s, j, pl.ds(pl.multiple_of(h * N, N), N), :] = jax.nn.gelu(hidden, approximate=True).astype(BF16)
            gather_start(act_rows(j), N, sems(ac_send, s, j), sems(ac_recv, s, j))
            yield
        for j in range(J):
            gather_relay(act_rows(j), N, sems(ac_send, s, j), sems(ac_recv, s, j))
            yield
        if s == 0:
            local[5].wait()
            arrived(wd.at[1 - c], w_recv.at[3])
        accs = [None] * C
        for j in range(J):
            gather_end(act_rows(j), N, sems(ac_recv, s, j))
            for cc in range(C):
                part = jnp.dot(act_rx[s, j], wd[cc, FW * j:FW * (j + 1), :], preferred_element_type=F32)
                accs[cc] = part if j == 0 else accs[cc] + part
                if j == J - 1:
                    ff_tx[s, cc] = accs[cc].astype(BF16)
                    to_owners(s, ff_tx, ff_rx, ff_send, ff_recv, cc)
            yield
        feed = from_owners(s, ff_rx, ff_recv)
        out[mine, :] = mix[mine, :] + modv[5:6, own_cols] * feed

    steps = [part_steps(s) for s in range(S)]
    for s in ORDER:
        next(steps[s], None)

    for s in range(S):

        @pl.when(u == c * H + h)
        def _():
            for copy in fix_copies(s):
                copy.wait_send()

    for own, copy in pending:
        if own is None:
            copy.wait_send()
        else:
            pl.when(jnp.logical_not(own))(copy.wait_send)


def on_device(
    tokens, cond, mod_weight, qkv_weight, q_gain, k_gain, out_weight, up_weight, down_weight
):
    U = lax.axis_size("ulysses")
    B = lax.axis_size("blk")
    T = lax.axis_size("tensor")
    H = T // 2
    R, W = tokens.shape
    G = H * R
    FFL = up_weight.shape[1]
    J = 2
    S = 2
    N = R // S
    dma = pltpu.SemaphoreType.DMA
    vmem = pltpu.VMEM
    any_spec = pl.BlockSpec(memory_space=pltpu.HBM)
    vm_spec = pl.BlockSpec(memory_space=pltpu.VMEM)
    return pl.pallas_call(
        functools.partial(block_kernel, U, B, T),
        out_shape=jax.ShapeDtypeStruct((R, W), F32),
        in_specs=[any_spec] * 9,
        out_specs=vm_spec,
        scratch_shapes=[
            vmem((R, W), BF16),
            vmem((mod_weight.shape[0] // 128, 128), BF16),
            vmem((1, 128), F32),
            vmem((1, 128), F32),
            vmem((2, G, W), BF16),
            vmem((mod_weight.shape[1], mod_weight.shape[0]), BF16),
            vmem((3, 2, W, W), BF16),
            vmem((2, W, W), BF16),
            vmem((2, W, FFL), BF16),
            vmem((2, FFL, W), BF16),
            vmem((8, 128), F32),
            vmem((B, 8, 128), F32),
            vmem((24, 128), F32),
            vmem((T, 24, 128), F32),
            vmem((24, 128), F32),
            vmem((U, 24, 128), F32),
            vmem((8, 2 * W), F32),
            vmem((8, G), F32),
            vmem((H, 8, G), F32),
            vmem((3, G, W), BF16),
            vmem((3, 2, R // 2, W), BF16),
            vmem((3, 2, R, W), BF16),
            vmem((S, B * N, W), BF16),
            vmem((2, T * R, W), BF16),
            vmem((S, B * N, W), BF16),
            vmem((S, B, N, W), BF16),
            vmem((S, B * N // 128, 8, 128), F32),
            vmem((S, B, 8, 128), F32),
            vmem((128, 128), F32),
            vmem((128, 128), F32),
            vmem((S, H * N, W), BF16),
            vmem((S, 2, H * N, W), BF16),
            vmem((S, U, N, W), BF16),
            vmem((R, W), F32),
            vmem((S, 8, 128), F32),
            vmem((S, T, 8, 128), F32),
            vmem((S, 16, 128), F32),
            vmem((S, 16, 128), F32),
            vmem((8, FFL), F32),
            vmem((H, 8, FFL), F32),
            vmem((S, N, W), BF16),
            vmem((S, 2, H * N, W), BF16),
            vmem((S, J, H * N, FFL // J), BF16),
            vmem((S, J, 2, N // 2, FFL // J), BF16),
            vmem((S, J, 2, N, FFL // J), BF16),
            vmem((S, J, H * N, FFL // J), BF16),
            vmem((S, 2, H * N, W), BF16),
            vmem((S, U, N, W), BF16),
            dma((9,)), dma((4,)), dma((4,)),
            dma((U,)), dma((2, H)), dma((B,)), dma((B,)), dma((T,)), dma((T,)), dma((U,)), dma((U,)),
            dma((H,)), dma((H,)), dma((3, H)), dma((3, H)), dma((S, B)), dma((S, B)),
            dma((2, H)), dma((2, H)), dma((2, H)), dma((2, H)), dma((S, B)), dma((S, B)), dma((S, B)), dma((S, B)),
            dma((S, H)), dma((S, H)), dma((S, 2, H)), dma((S, U)), dma((S, T)), dma((S, T)), dma((S, U)), dma((S,)), dma((H,)), dma((H,)), dma((S, U)), dma((S, 2, H)),
            dma((S, J, H)), dma((S, J, H)), dma((S, J, H)), dma((S, J, H)), dma((S, 2, H)), dma((S, U)),
        ],
        compiler_params=pltpu.CompilerParams(
            collective_id=0, has_side_effects=True, vmem_limit_bytes=67043328
        ),
        name="block_kernel",
    )(
        tokens,
        cond.reshape(-1, 128),
        mod_weight.T,
        qkv_weight.transpose(1, 0, 2),
        q_gain.reshape(1, -1),
        k_gain.reshape(1, -1),
        out_weight,
        up_weight,
        down_weight,
    )


def solution(mesh):
    return jax.shard_map(
        on_device,
        mesh=mesh,
        in_specs=(
            P(("ulysses", "blk"), "tensor"),
            P(),
            P(None, ("ulysses", "blk", "tensor")),
            P("tensor", None, "ulysses"),
            P(),
            P(),
            P("ulysses", "tensor"),
            P("tensor", "ulysses"),
            P("ulysses", "tensor"),
        ),
        out_specs=P(("ulysses", "blk"), "tensor"),
        check_vma=False,
    )
```

time: 137 us -> 130 us (0.949)
  Pallas kernels: 135 us -> 128 us
    pallas_call x1, Pallas kernels: 135 us -> 128 us  [on_device(): pl.pallas_call(functools.partial(block_kernel, U, B, T), out_shape=jax.Sh...]
where the time goes in v3:
time: 130 us; the launch traced here: 129 us
  Pallas kernels  128 us (98%)
  local copies, waits for them, and re-layouts  1.54 us (1%)
    pallas_call x1, Pallas kernels, on_device(): pl.pallas_call(functools.partial(block_kernel, U, B, T), out_shape=jax.Sh...  128 us

profile of v3, /device:TPU:1, one launch (start us, length us, event | category | flops | bytes accessed | tf_op | source)
XLA Modules:
  0.0 129.5 jit_solution(13905517806423285252)
XLA Ops:
  0.0 127.9 %block_kernel.1 = f32[64,384]{1,0:T(8,128)} custom-call(bf16[64,384]{1,0:T(8,128)(2,1)} %tokens.1, bf16[24,128]{1,0:T(8,128)(2,1)} %bitcast.7, bf16[36,3072]{1,0:T(8,128)(2,1)} %bitcast.6, bf16[3,384,384]{2,1,0:T(8,128)(2,1)} %bitcast.5, f32[1,128]{1,0:T(1,128)} %bitcast.8, f32[1,128]{1,0:T(1,128)} %bitcast.9, bf16[384,384]{1,0:T(8,128)(2,1)} %out_w.1, ...), custom_call_target="tpu_custom_call" | custom-call | tf_op jit(solution)/shard_map/block_kernel/pallas_call | solution.py:601
  127.9 1.5 %copy.11 = f32[64,384]{1,0:T(8,128)} copy(f32[64,384]{1,0:T(8,128)} %block_kernel.1) | data formatting | bytes 196608

commit v4 on v3

--- a/solution.py
+++ b/solution.py
@@ -100,10 +100,16 @@
         arrived(rows(ho, 0, half), recv(2))
         arrived(rows(ho, half, half), recv(3))
 
-    def scatter_start(tx, rb, n, send, recv):
+    def scatter_start(tx, rb, rx, n, send, recv):
         half = n // 2
         rdma(tx.at[pl.ds(ho * n, half), :], rb.at[0], send(0), recv(0), right)
         rdma(tx.at[pl.ds(ho * n + half, half), :], rb.at[1], send(1), recv(1), left)
+        for side, (to, dev) in enumerate(((hr, right), (hl, left))):
+            lo = (1 - side) * half
+            rdma(
+                tx.at[pl.ds(to * n + lo, half), :], rx.at[side, pl.ds(lo, half), :],
+                send(4 + side), recv(4 + side), dev,
+            )
 
     def scatter_relay(tx, rb, rx, n, send, recv):
         half = n // 2
@@ -111,11 +117,16 @@
             arrived(rb.at[side], recv(side))
             at = pl.ds(pl.multiple_of(to * n + side * half, half), half)
             tx[at, :] = (tx[at, :].astype(F32) + rb[side].astype(F32)).astype(BF16)
-            rdma(tx.at[pl.ds(to * n, n), :], rx.at[side], send(2 + side), recv(2 + side), dev)
+            rdma(
+                tx.at[pl.ds(to * n + side * half, half), :], rx.at[side, pl.ds(side * half, half), :],
+                send(2 + side), recv(2 + side), dev,
+            )
 
     def scatter_end(tx, rx, n, recv):
-        arrived(rx.at[0], recv(2))
-        arrived(rx.at[1], recv(3))
+        half = n // 2
+        for side in range(2):
+            arrived(rx.at[side, pl.ds((1 - side) * half, half), :], recv(4 + side))
+            arrived(rx.at[side, pl.ds(side * half, half), :], recv(2 + side))
         own = tx[pl.ds(pl.multiple_of(h * n, n), n), :].astype(F32)
         return own + rx[0].astype(F32) + rx[1].astype(F32)
 
@@ -265,7 +276,7 @@
         part = jnp.dot(n0, wq[g, 0], preferred_element_type=F32)
         part = part + jnp.dot(n1, wq[g, 1], preferred_element_type=F32)
         rs_tx[g] = part.astype(BF16)
-        scatter_start(rs_tx.at[g], rs_rb.at[g], R, rs_sems(rs_send, g), rs_sems(rs_recv, g))
+        scatter_start(rs_tx.at[g], rs_rb.at[g], rs_rx.at[g], R, rs_sems(rs_send, g), rs_sems(rs_recv, g))
 
     heads = W // 128
 
@@ -491,7 +502,7 @@
             part = jnp.dot(n2_rx[s, 0], wu[0, :, cut], preferred_element_type=F32)
             part = part + jnp.dot(n2_rx[s, 1], wu[1, :, cut], preferred_element_type=F32)
             up_tx[s, j] = part.astype(BF16)
-            scatter_start(up_tx.at[s, j], up_rb.at[s, j], N, sems(up_send, s, j), sems(up_recv, s, j))
+            scatter_start(up_tx.at[s, j], up_rb.at[s, j], up_rx.at[s, j], N, sems(up_send, s, j), sems(up_recv, s, j))
         yield
         for k in range(1, T):
             tp = lax.rem(t + k, T)
@@ -654,10 +665,10 @@
             vmem((S, U, N, W), BF16),
             dma((9,)), dma((4,)), dma((4,)),
             dma((U,)), dma((2, H)), dma((B,)), dma((B,)), dma((T,)), dma((T,)), dma((U,)), dma((U,)),
-            dma((H,)), dma((H,)), dma((3, H)), dma((3, H)), dma((S, B)), dma((S, B)),
+            dma((H,)), dma((H,)), dma((3, 6)), dma((3, 6)), dma((S, B)), dma((S, B)),
             dma((2, H)), dma((2, H)), dma((2, H)), dma((2, H)), dma((S, B)), dma((S, B)), dma((S, B)), dma((S, B)),
             dma((S, H)), dma((S, H)), dma((S, 2, H)), dma((S, U)), dma((S, T)), dma((S, T)), dma((S, U)), dma((S,)), dma((H,)), dma((H,)), dma((S, U)), dma((S, 2, H)),
-            dma((S, J, H)), dma((S, J, H)), dma((S, J, H)), dma((S, J, H)), dma((S, 2, H)), dma((S, U)),
+            dma((S, J, 6)), dma((S, J, 6)), dma((S, J, H)), dma((S, J, H)), dma((S, 2, H)), dma((S, U)),
         ],
         compiler_params=pltpu.CompilerParams(
             collective_id=0, has_side_effects=True, vmem_limit_bytes=67043328

time: 130 us -> 131 us (level)
  Pallas kernels: 128 us -> 130 us
    pallas_call x1, Pallas kernels: 128 us -> 130 us  [on_device(): pl.pallas_call(functools.partial(block_kernel, U, B, T), out_shape=jax.Sh...]
where the time goes in v4:
time: 131 us
  Pallas kernels  130 us (99%)
  local copies, waits for them, and re-layouts  1.54 us (1%)
    pallas_call x1, Pallas kernels, on_device(): pl.pallas_call(functools.partial(block_kernel, U, B, T), out_shape=jax.Sh...  130 us

profile of v4, /device:TPU:1, one launch (start us, length us, event | category | flops | bytes accessed | tf_op | source)
XLA Modules:
  0.0 131.3 jit_solution(16989016434954730695)
XLA Ops:
  0.0 129.7 %block_kernel.1 = f32[64,384]{1,0:T(8,128)} custom-call(bf16[64,384]{1,0:T(8,128)(2,1)} %tokens.1, bf16[24,128]{1,0:T(8,128)(2,1)} %bitcast.7, bf16[36,3072]{1,0:T(8,128)(2,1)} %bitcast.6, bf16[3,384,384]{2,1,0:T(8,128)(2,1)} %bitcast.5, f32[1,128]{1,0:T(1,128)} %bitcast.8, f32[1,128]{1,0:T(1,128)} %bitcast.9, bf16[384,384]{1,0:T(8,128)(2,1)} %out_w.1, ...), custom_call_target="tpu_custom_call" | custom-call | tf_op jit(solution)/shard_map/block_kernel/pallas_call | solution.py:612
  129.7 1.5 %copy.11 = f32[64,384]{1,0:T(8,128)} copy(f32[64,384]{1,0:T(8,128)} %block_kernel.1) | data formatting | bytes 196608

commit v5 on v3

--- a/solution.py
+++ b/solution.py
@@ -8,7 +8,7 @@
 from jax.experimental.pallas import tpu as pltpu
 from jax.sharding import PartitionSpec as P
 
-ORDER = [int(s) for s in "01001010101001010011010101011101"]
+ORDER = [int(s) for s in "01001011010010100101010101011101"]
 MESH = pl.DeviceIdType.MESH
 F32 = jnp.float32
 BF16 = jnp.bfloat16

time: 130 us -> 129 us (level)
  no operation moved by 1% of the time
where the time goes in v5:
time: 129 us
  Pallas kernels  127 us (98%)
  local copies, waits for them, and re-layouts  1.54 us (1%)
    pallas_call x1, Pallas kernels, on_device(): pl.pallas_call(functools.partial(block_kernel, U, B, T), out_shape=jax.Sh...  127 us

profile of v5, /device:TPU:1, one launch (start us, length us, event | category | flops | bytes accessed | tf_op | source)
XLA Modules:
  0.0 128.9 jit_solution(7447659217974782541)
XLA Ops:
  0.0 127.4 %block_kernel.1 = f32[64,384]{1,0:T(8,128)} custom-call(bf16[64,384]{1,0:T(8,128)(2,1)} %tokens.1, bf16[24,128]{1,0:T(8,128)(2,1)} %bitcast.7, bf16[36,3072]{1,0:T(8,128)(2,1)} %bitcast.6, bf16[3,384,384]{2,1,0:T(8,128)(2,1)} %bitcast.5, f32[1,128]{1,0:T(1,128)} %bitcast.8, f32[1,128]{1,0:T(1,128)} %bitcast.9, bf16[384,384]{1,0:T(8,128)(2,1)} %out_w.1, ...), custom_call_target="tpu_custom_call" | custom-call | tf_op jit(solution)/shard_map/block_kernel/pallas_call | solution.py:601
  127.4 1.5 %copy.11 = f32[64,384]{1,0:T(8,128)} copy(f32[64,384]{1,0:T(8,128)} %block_kernel.1) | data formatting | bytes 196608
